TPU v7x, 128 devices: a whole 4x4x4 slice. The times are simulated.
128 devices in a mesh: gx: 16 (over z, y), gy: 8 (over x, core).
Axes of the slice: x: 4, y: 4, z: 4, core: 2. Of those that a mesh axis runs over, the one named last changes fastest.
Arguments:
- object_field: float32 [2, 4096, 8192], P(None, 'gy', 'gx'), may hold values from -6 to 6
- probe: float32 [2, 256, 256], replicated, may hold values from -4 to 4
- frames: float32 [8, 16, 16, 2, 256, 256], P('gy', 'gx'), may hold values from 0.2 to 5
- positions: int32 [8, 16, 24, 2], P('gy', 'gx'), may hold values from -128 to 384
- helpers: int32 [8, 16, 24, 1], P('gy', 'gx'), may hold values from 0 to 15; in each aligned block of 24 rows (0 to 23, 24 to 47, ..., all dimensions but the last counted through in order) at most 2 rows name the same one
- task_counts: int32 [8, 16], P('gy', 'gx'), may hold values from 6 to 24, as said below
Outputs:
- updated_field: float32 [2, 4096, 8192], P(None, 'gy', 'gx')
Inputs may be any that keep to these rules, and one draw needn't show every extreme that they name: `helpers`: among one tile's 24 task slots no helper column is named more than 2 times, and in some tiles one is named exactly 2 times. `task_counts`: some tile has all 24 tasks valid.
All inputs are finite; a program needn't handle non-finite values.
Results may differ from a plain program's by a relative error of at most 0.0003.
Values sent between devices are 32-bit elements; how exact they have to be, the bound alone decides.
No kernel may reach another device: no remote copies, remote signals or barrier semaphores. Data moves between devices by JAX's collectives and lax.ppermute only.
A program may use at most 192 MiB of HBM per device.

v0:
```python
import jax
import jax.numpy as jnp
from jax import lax
from jax.sharding import PartitionSpec as P

PATCH = 256
TASKS = 24


step_size = 0.1
ridge = 0.5


def extended_2(block, sides, width):
    for axis, dim in sides:
        count = lax.axis_size(axis)
        forward = [(i, i + 1) for i in range(count - 1)]
        backward = [(target, source) for source, target in forward]
        low = lax.ppermute(
            lax.slice_in_dim(block, block.shape[dim] - width, None, axis=dim), axis, forward
        )
        high = lax.ppermute(lax.slice_in_dim(block, 0, width, axis=dim), axis, backward)
        block = jnp.concatenate([low, block, high], axis=dim)
    return block


def dft_tables(length):
    index = jnp.arange(length, dtype=jnp.int32)
    phase = index[:, None] * index[None, :] % length
    angle = 2.0 * jnp.pi / length * phase.astype(jnp.float32)
    factor = length ** (-0.5)
    return (jnp.cos(angle) * factor, -jnp.sin(angle) * factor)


def right_mul(real_in, imag_in, table_re, table_im):
    highest = lax.Precision.HIGHEST
    first = jnp.einsum("bij,jk->bik", real_in, table_re, precision=highest)
    second = jnp.einsum("bij,jk->bik", imag_in, table_im, precision=highest)
    third = jnp.einsum("bij,jk->bik", real_in + imag_in, table_re + table_im, precision=highest)
    return (first - second, third - first - second)


def left_mul(table_re, table_im, real_in, imag_in):
    highest = lax.Precision.HIGHEST
    first = jnp.einsum("ij,bjk->bik", table_re, real_in, precision=highest)
    second = jnp.einsum("ij,bjk->bik", table_im, imag_in, precision=highest)
    third = jnp.einsum("ij,bjk->bik", table_re + table_im, real_in + imag_in, precision=highest)
    return (first - second, third - first - second)


def transform(real_in, imag_in, table_re, table_im):
    mid_re, mid_im = right_mul(real_in, imag_in, table_re, table_im)
    return left_mul(table_re, table_im, mid_re, mid_im)


def task_grad(patches, measured, probe):
    length = patches.shape[-1]
    table_re, table_im = dft_tables(length)
    probe_re, probe_im = (probe[0], probe[1])
    obj_re, obj_im = (patches[:, 0], patches[:, 1])
    wave_re = probe_re * obj_re - probe_im * obj_im
    wave_im = probe_re * obj_im + probe_im * obj_re
    far_re, far_im = transform(wave_re, wave_im, table_re, table_im)
    weight = far_re * far_re + far_im * far_im - measured
    back_re, back_im = transform(weight * far_re, weight * far_im, table_re, -table_im)
    grad_re = probe_re * back_re + probe_im * back_im
    grad_im = probe_re * back_im - probe_im * back_re
    return jnp.stack([grad_re, grad_im], axis=1)


def per_device(object_field, probe, frames, positions, helpers, task_counts):
    tile = object_field.shape[1]
    half = PATCH // 2
    zero = jnp.int32(0)
    extended = extended_2(object_field, (("gx", 2), ("gy", 1)), half)
    offsets = positions[0, 0]
    task_ids = jnp.arange(TASKS, dtype=jnp.int32)
    valid = task_ids < task_counts[0, 0]
    helper_cols = helpers[0, 0, :, 0]
    same = helper_cols[:, None] == helper_cols[None, :]
    ranks = jnp.sum(jnp.logical_and(same, task_ids[None, :] < task_ids[:, None]), axis=1)
    kept = frames[0, 0]
    sources = kept.shape[0]
    slot_count = kept.shape[1]
    width_all = sources * slot_count
    slot_of = helper_cols * slot_count + ranks

    def cut_patch(offset):
        return lax.dynamic_slice(
            extended, (zero, offset[0] + half, offset[1] + half), (2, PATCH, PATCH)
        )

    live = valid.astype(jnp.float32)[:, None, None, None]
    patches = jax.vmap(cut_patch)(offsets) * live
    slot_ids = jnp.arange(width_all, dtype=jnp.int32)
    match = jnp.logical_and(slot_of[None, :] == slot_ids[:, None], valid[None, :])
    filler = jnp.argmax(match, axis=1)
    filled = jnp.any(match, axis=1)
    outgoing = jnp.where(filled[:, None, None, None], patches[filler], 0.0)
    outgoing = outgoing.reshape(sources, slot_count, 2, PATCH, PATCH)
    arrived = lax.all_to_all(outgoing, "gx", split_axis=0, concat_axis=0, tiled=True)
    worked = task_grad(
        arrived.reshape(width_all, 2, PATCH, PATCH), kept.reshape(width_all, PATCH, PATCH), probe
    )
    returned = lax.all_to_all(
        worked.reshape(sources, slot_count, 2, PATCH, PATCH),
        "gx",
        split_axis=0,
        concat_axis=0,
        tiled=True,
    )
    grads = returned.reshape(width_all, 2, PATCH, PATCH)[slot_of]
    grads = grads * live

    def add_patch(index, total):
        start_y = offsets[index, 0] + half
        start_x = offsets[index, 1] + half
        current = lax.dynamic_slice(total, (zero, start_y, start_x), (2, PATCH, PATCH))
        return lax.dynamic_update_slice(total, current + grads[index], (zero, start_y, start_x))

    summed = lax.fori_loop(
        0, TASKS, add_patch, jnp.zeros((2, tile + 2 * half, tile + 2 * half), jnp.float32)
    )
    side_cols = jnp.zeros((2, tile + 2 * half, tile), jnp.float32)
    side_cols = side_cols.at[:, :, :half].set(summed[:, :, :half])
    side_cols = side_cols.at[:, :, tile - half :].set(summed[:, :, tile + half :])
    beside = extended_2(side_cols, (("gx", 2),), half)
    middle = summed[:, :, half : half + tile]
    middle = middle.at[:, :, :half].add(beside[:, :, :half])
    middle = middle.at[:, :, tile - half :].add(beside[:, :, tile + half :])
    side_rows = jnp.zeros((2, tile, tile), jnp.float32)
    side_rows = side_rows.at[:, :half, :].set(middle[:, :half, :])
    side_rows = side_rows.at[:, tile - half :, :].set(middle[:, tile + half :, :])
    above = extended_2(side_rows, (("gy", 1),), half)
    gradient = middle[:, half : half + tile, :]
    gradient = gradient.at[:, :half, :].add(above[:, :half, :])
    gradient = gradient.at[:, tile - half :, :].add(above[:, tile + half :, :])
    return object_field - step_size * (gradient + ridge * object_field)


def solution(mesh):
    in_specs = (
        P(None, "gy", "gx"),
        P(),
        P("gy", "gx", None, None, None, None),
        P("gy", "gx", None, None),
        P("gy", "gx", None, None),
        P("gy", "gx"),
    )
    out_specs = P(None, "gy", "gx")
    return jax.shard_map(
        per_device, mesh=mesh, in_specs=in_specs, out_specs=out_specs, check_vma=False
    )
```

profile of v0, /device:TPU:91, one launch (start us, length us, event | category | flops | bytes accessed | tf_op | source)
XLA Modules:
  0.0 1352.1 jit_solution(17656706540598842470)
XLA Ops:
  41.5 100.1 %while.26 = (s32[]{:T(128)}, f32[2,768,768]{2,1,0:T(8,128)}, s32[24,3]{0,1:T(4,128)S(1)}, f32[24,2,256,256]{3,2,1,0:T(8,128)}, s32[]{:T(128)}) while((s32[]{:T(128)}, f32[2,768,768]{2,1,0:T(8,128)}, s32[24,3]{0,1:T(4,128)S(1)}, f32[24,2,256,256]{3,2,1,0:T(8,128)}, s32[]{:T(128)}) %tuple.99), condition=%wide.while_cond.8, body=%wide.while_body.8.sunk | while | flops 2 | bytes 1050217 | solution.py:89
  152.5 12.7 gather_fusion
  165.2 17.7 %copy.61 = f32[16,2,2,256,256]{3,4,1,2,0:T(8,128)} copy(f32[16,2,2,256,256]{4,3,2,1,0:T(8,128)} %bitcast.163) | data formatting | bytes 33554432 | tf_op jit(solution)/shard_map/gather | solution.py:99
  182.9 11.6 broadcast_select_fusion
  211.3 236.4 %all-to-all-done = f32[16,2,2,256,256]{3,4,1,2,0:T(8,128)} async-done(((f32[16,2,2,256,256]{3,4,1,2,0:T(8,128)}), f32[16,2,2,256,256]{3,4,1,2,0:T(8,128)}, u32[]{:S(2)}, u32[]{:S(2)}) %all-to-all-start) | async-done | bytes 16777248 | tf_op jit(solution)/shard_map/all_to_all | solution.py:101
  447.8 11.5 copy.62
  459.3 19.8 %fusion.26 = f32[32,256,256]{2,1,0:T(8,128)S(1)} fusion(f32[32,2,256,256]{2,3,0,1:T(8,128)} %bitcast.160, f32[256,256]{0,1:T(8,128)S(1)} %copy.63, f32[256,256]{0,1:T(8,128)S(1)} %copy.60), kind=kOutput, calls=%fused_computation.44 | convolution fusion | flops 6449725440 | bytes 25690112 | tf_op jit(solution)/shard_map/bij,jk->bik/dot_general | solution.py:37
  479.1 23.9 %fusion.27 = f32[32,256,256]{2,1,0:T(8,128)} fusion(f32[32,2,256,256]{2,3,0,1:T(8,128)} %bitcast.161, f32[256,256]{0,1:T(8,128)S(1)} %copy.63, f32[256,256]{0,1:T(8,128)S(1)} %copy.60), kind=kOutput, calls=%fused_computation.45 | convolution fusion | flops 6449790976 | bytes 25690112 | tf_op jit(solution)/shard_map/bij,jk->bik/dot_general | solution.py:38
  503.0 23.6 %subtract_subtract_fusion.1 = f32[32,256,256]{2,1,0:T(8,128)} fusion(f32[32,256,256]{2,1,0:T(8,128)} %fusion.27, f32[32,256,256]{2,1,0:T(8,128)S(1)} %fusion.26, f32[32,2,256,256]{2,3,0,1:T(8,128)} %bitcast.162, f32[256,256]{0,1:T(8,128)S(1)} %copy.63, f32[256,256]{0,1:T(8,128)S(1)} %copy.60), kind=kOutput, calls=%fused_computation.28 | convolution fusion | flops 6462504960 | bytes 42467328 | tf_op jit(solution)/shard_map/bij,jk->bik/dot_general | solution.py:39
  526.6 19.8 %fusion.16 = f32[32,256,256]{2,1,0:T(8,128)} fusion(f32[32,256,256]{2,1,0:T(8,128)S(1)} %fusion.26, f32[32,256,256]{2,1,0:T(8,128)} %fusion.27), kind=kOutput, calls=%fused_computation.41 | convolution fusion | flops 6445531136 | bytes 25165824 | tf_op jit(solution)/shard_map/ij,bjk->bik/dot_general | solution.py:45
  546.4 17.9 %fusion.42 = f32[32,256,256]{2,1,0:T(8,128)} fusion(f32[32,256,256]{2,1,0:T(8,128)S(1)} %copy-done.3), kind=kOutput, calls=%fused_computation.69 | convolution fusion | flops 6443499520 | bytes 16777216 | tf_op jit(solution)/shard_map/ij,bjk->bik/dot_general | solution.py:46
  564.3 29.4 %fusion.7 = (f32[32,256,256]{1,2,0:T(8,128)}, f32[32,256,256]{1,2,0:T(8,128)}) fusion(f32[1,1,16,2,256,256]{4,5,3,2,1,0:T(8,128)} %copy.70, f32[32,256,256]{2,1,0:T(8,128)} %fusion.42, f32[32,256,256]{2,1,0:T(8,128)} %fusion.16, f32[32,256,256]{2,1,0:T(8,128)} %subtract_subtract_fusion.1, f32[32,256,256]{2,1,0:T(8,128)} %copy-done.1, ...), kind=kOutput, calls=%fused_computation.25 | convolution fusion | flops 6466699264 | bytes 67108864 | tf_op jit(solution)/shard_map/ij,bjk->bik/dot_general | solution.py:47
  593.7 19.1 %fusion.38 = f32[32,256,256]{2,1,0:T(8,128)S(1)} fusion(f32[32,256,256]{1,2,0:T(8,128)} %get-tuple-element.257), kind=kOutput, calls=%fused_computation.65 | convolution fusion | flops 6443565056 | bytes 16777216 | tf_op jit(solution)/shard_map/bij,jk->bik/dot_general | solution.py:38
  612.9 14.3 %fusion.46 = f32[32,256,256]{2,1,0:T(8,128)S(1)} fusion(f32[32,256,256]{1,2,0:T(8,128)S(1)} %copy-done.2), kind=kOutput, calls=%fused_computation.73 | convolution fusion | flops 6443433984 | bytes 16777216 | tf_op jit(solution)/shard_map/bij,jk->bik/dot_general | solution.py:37
  630.4 17.1 %fusion.13 = f32[32,256,256]{2,1,0:T(8,128)} fusion(f32[32,256,256]{2,1,0:T(8,128)S(1)} %fusion.46, f32[32,256,256]{2,1,0:T(8,128)S(1)} %fusion.38), kind=kOutput, calls=%fused_computation.38 | convolution fusion | flops 6445531136 | bytes 25165824 | tf_op jit(solution)/shard_map/ij,bjk->bik/dot_general | solution.py:45
  647.5 22.6 %subtract_subtract_fusion = f32[32,256,256]{2,1,0:T(8,128)} fusion(f32[32,256,256]{2,1,0:T(8,128)S(1)} %fusion.38, f32[32,256,256]{2,1,0:T(8,128)} %copy-done, f32[32,256,256]{1,2,0:T(8,128)} %get-tuple-element.256, f32[32,256,256]{1,2,0:T(8,128)} %get-tuple-element.257), kind=kOutput, calls=%fused_computation.21 | convolution fusion | flops 6449987584 | bytes 41943040 | tf_op jit(solution)/shard_map/bij,jk->bik/dot_general | solution.py:39
  670.1 19.6 %fusion.36 = f32[32,256,256]{2,1,0:T(8,128)} fusion(f32[32,256,256]{2,1,0:T(8,128)} %subtract_subtract_fusion), kind=kOutput, calls=%fused_computation.63 | convolution fusion | flops 6443565056 | bytes 16777216 | tf_op jit(solution)/shard_map/ij,bjk->bik/dot_general | solution.py:46
  689.8 26.2 %multiply_add_fusion = (f32[32,256,256]{1,2,0:T(8,128)}, f32[32,256,256]{1,2,0:T(8,128)}) fusion(f32[256,256]{0,1:T(8,128)S(1)} %copy.63, f32[256,256]{0,1:T(8,128)S(1)} %copy.60, f32[32,256,256]{2,1,0:T(8,128)} %fusion.36, f32[32,256,256]{2,1,0:T(8,128)} %fusion.13, f32[32,256,256]{2,1,0:T(8,128)} %subtract_subtract_fusion, f32[32,256,256]{2,1,0:T(8,128)} %copy-done, ...), kind=kOutput, calls=%fused_computation.18 | convolution fusion | flops 6466764800 | bytes 59244544 | tf_op jit(solution)/shard_map/ij,bjk->bik/dot_general | solution.py:47
  716.0 11.6 pad_maximum_fusion
  738.1 247.1 %all-to-all-done.1 = f32[16,2,2,256,256]{3,4,1,2,0:T(8,128)} async-done(((f32[16,2,2,256,256]{3,4,1,2,0:T(8,128)}), f32[16,2,2,256,256]{3,4,1,2,0:T(8,128)}, u32[]{:S(2)}, u32[]{:S(2)}) %all-to-all-start.1) | async-done | bytes 16777248 | tf_op jit(solution)/shard_map/all_to_all | solution.py:105
  985.2 17.7 %copy.79 = f32[16,2,2,256,256]{4,3,2,1,0:T(8,128)} copy(f32[16,2,2,256,256]{3,4,1,2,0:T(8,128)} %all-to-all-done.1) | data formatting | bytes 33554432 | tf_op jit(solution)/shard_map/all_to_all | solution.py:105
  1002.9 12.9 gather_fusion.1
  1029.1 275.0 %while.25 = (s32[]{:T(128)}, f32[2,768,768]{2,1,0:T(8,128)}, s32[24,2]{0,1:T(2,128)S(1)}, f32[24,2,256,256]{3,2,1,0:T(8,128)}, s32[]{:T(128)}, /*index=5*/s32[1,1]{0,1:T(1,128)}, s32[]{:T(128)}, s32[1,1]{0,1:T(1,128)}) while((s32[]{:T(128)}, f32[2,768,768]{2,1,0:T(8,128)}, s32[24,2]{0,1:T(2,128)S(1)}, f32[24,2,256,256]{3,2,1,0:T(8,128)}, ...), condition=%wide.region_4.5_spmd, body=%wide.region_3.4_spmd.sunk | while | flops 131082 | bytes 2621653 | solution.py:121
  1314.6 11.9 collective-permute-done.4
  (227 shorter events, 443.3 us)
Async XLA Ops:
  0.0 27.7 %copy-start.6 = (s32[1,1,24,2]{2,3,1,0:T(2,128)S(1)}, s32[1,1,24,2]{2,3,1,0:T(2,128)}, u32[]{:S(2)}) copy-start(s32[1,1,24,2]{2,3,1,0:T(2,128)} %param.27) | copy-start | bytes 580
  1.3 14.7 %collective-permute-start = (f32[2,512,128]{2,1,0:T(8,128)S(1)}, f32[2,512,128]{2,1,0:T(8,128)S(1)}, u32[]{:S(2)}, u32[]{:S(2)}) collective-permute-start(f32[2,512,128]{2,1,0:T(8,128)S(1)} %get-tuple-element.267), channel_id=1, source_target_pairs={{0,8},{8,16},{16,24},{24,32},{32,40},{40,48},{48,56},{56,64},{64,7... | collective-permute-start | bytes 1572872 | tf_op jit(solution)/shard_map/ppermute | solution.py:19
  4.2 16.5 %collective-permute-start.1 = (f32[2,512,128]{2,1,0:T(8,128)S(1)}, f32[2,512,128]{2,1,0:T(8,128)S(1)}, u32[]{:S(2)}, u32[]{:S(2)}) collective-permute-start(f32[2,512,128]{2,1,0:T(8,128)S(1)} %get-tuple-element.266), channel_id=1, source_target_pairs={{8,0},{16,8},{24,16},{32,24},{40,32},{48,40},{56,48},{64,56},{72,6... | collective-permute-start | bytes 1572872 | tf_op jit(solution)/shard_map/ppermute | solution.py:22
  7.5 1.3 copy-start.12
  8.8 132.7 %copy-start.9 = (f32[24]{0:T(128)}, f32[24]{0:T(128)S(1)}, u32[]{:S(2)}) copy-start(f32[24]{0:T(128)S(1)} %get-tuple-element.273) | copy-start | bytes 292
  20.9 13.7 %collective-permute-start.2 = (f32[2,128,768]{2,1,0:T(8,128)S(1)}, f32[2,128,768]{2,1,0:T(8,128)S(1)}, u32[]{:S(2)}, u32[]{:S(2)}) collective-permute-start(f32[2,128,768]{2,1,0:T(8,128)S(1)} %get-tuple-element.264), channel_id=1, source_target_pairs={{0,1},{1,2},{2,3},{3,4},{4,5},{5,6},{6,7},{8,9},{9,10},{10,11},{11... | collective-permute-start | bytes 2359304 | tf_op jit(solution)/shard_map/ppermute | solution.py:19
  25.7 13.3 collective-permute-start.3
  194.5 7.2 copy-start.5
  194.5 253.3 %all-to-all-start = ((f32[16,2,2,256,256]{3,4,1,2,0:T(8,128)}), f32[16,2,2,256,256]{3,4,1,2,0:T(8,128)}, u32[]{:S(2)}, u32[]{:S(2)}) async-start(f32[16,2,2,256,256]{3,4,1,2,0:T(8,128)} %broadcast_select_fusion), calls=%async_computation | async-start | bytes 33554432 | tf_op jit(solution)/shard_map/all_to_all | solution.py:101
  479.1 47.5 %copy-start.1 = (f32[32,256,256]{2,1,0:T(8,128)}, f32[32,256,256]{2,1,0:T(8,128)S(1)}, u32[]{:S(2)}) copy-start(f32[32,256,256]{2,1,0:T(8,128)S(1)} %fusion.26) | copy-start | bytes 25165828
  526.6 19.8 %copy-start.3 = (f32[32,256,256]{2,1,0:T(8,128)S(1)}, f32[32,256,256]{2,1,0:T(8,128)}, u32[]{:S(2)}) copy-start(f32[32,256,256]{2,1,0:T(8,128)} %subtract_subtract_fusion.1) | copy-start | bytes 25165828
  593.7 19.1 %copy-start.2 = (f32[32,256,256]{1,2,0:T(8,128)S(1)}, f32[32,256,256]{1,2,0:T(8,128)}, u32[]{:S(2)}) copy-start(f32[32,256,256]{1,2,0:T(8,128)} %get-tuple-element.256) | copy-start | bytes 25165828
  627.1 3.2 copy-start
  727.6 10.5 copy-start.11
  727.6 10.5 copy-start.13
  727.6 257.7 %all-to-all-start.1 = ((f32[16,2,2,256,256]{3,4,1,2,0:T(8,128)}), f32[16,2,2,256,256]{3,4,1,2,0:T(8,128)}, u32[]{:S(2)}, u32[]{:S(2)}) async-start(f32[16,2,2,256,256]{3,4,1,2,0:T(8,128)} %pad_maximum_fusion), calls=%async_computation.1 | async-start | bytes 33554432 | tf_op jit(solution)/shard_map/all_to_all | solution.py:105
  1002.9 12.9 copy-start.10
  1015.8 13.3 copy-start.7
  1304.1 8.4 copy-start.8
  1305.3 21.2 %collective-permute-start.4 = (f32[2,768,128]{2,1,0:T(8,128)S(1)}, f32[2,768,128]{2,1,0:T(8,128)S(1)}, u32[]{:S(2)}, u32[]{:S(2)}) collective-permute-start(f32[2,768,128]{2,1,0:T(8,128)S(1)} %slice.254), channel_id=1, source_target_pairs={{0,8},{8,16},{16,24},{24,32},{32,40},{40,48},{48,56},{56,64},{64,7... | collective-permute-start | bytes 2359304 | tf_op jit(solution)/shard_map/ppermute | solution.py:19
  1312.7 22.0 %collective-permute-start.5 = (f32[2,768,128]{2,1,0:T(8,128)S(1)}, f32[2,768,128]{2,1,0:T(8,128)S(1)}, u32[]{:S(2)}, u32[]{:S(2)}) collective-permute-start(f32[2,768,128]{2,1,0:T(8,128)S(1)} %slice_select_fusion), channel_id=1, source_target_pairs={{8,0},{16,8},{24,16},{32,24},{40,32},{48,40},{56,48},{64,56},{72,6... | collective-permute-start | bytes 2359304 | tf_op jit(solution)/shard_map/ppermute | solution.py:22
  1327.8 22.2 %copy-start.4 = (f32[2,512,512]{2,1,0:T(8,128)S(1)}, f32[2,512,512]{2,1,0:T(8,128)}, u32[]{:S(2)}) copy-start(f32[2,512,512]{2,1,0:T(8,128)} %param.24) | copy-start | bytes 6291460
  1334.9 9.9 collective-permute-start.6
  1339.3 10.5 collective-permute-start.7
where the time goes:
time: 1370 us; the launch traced here: 1350 us
  waiting for transfers between devices  531 us (39%)
  local copies, waits for them, and re-layouts  372 us (27%)
  matrix products  253 us (18%)
  other arithmetic  90.2 us (7%)
  loops' own time  62.9 us (5%)
  starting transfers between devices  41 us (3%)
    all_to_all x1, waiting for transfers between devices, per_device(): lax.all_to_all(worked.reshape(sources, slot_count, 2, PATCH, PATCH), 'gx'...  247 us
    all_to_all x1, waiting for transfers between devices, per_device(): lax.all_to_all(outgoing, 'gx', split_axis=0, concat_axis=0, tiled=True)  236 us
    dynamic_update_slice x24, local copies, waits for them, and re-layouts, add_patch(): lax.dynamic_update_slice(total, current + grads[index], (zero, start_y, s...  160 us
    gather x72, local copies, waits for them, and re-layouts  100 us
    another operation x1, loops' own time, per_device(): lax.fori_loop(0, TASKS, add_patch, jnp.zeros((2, tile + 2 * half, tile +...  62.9 us
    dot_general x2, matrix products, left_mul(): jnp.einsum('ij,bjk->bik', table_re + table_im, real_in + imag_in, precisi...  55.7 us
    dot_general x2, matrix products, right_mul(): jnp.einsum('bij,jk->bik', real_in + imag_in, table_re + table_im, precisi...  46.2 us
    dot_general x2, matrix products, right_mul(): second = jnp.einsum('bij,jk->bik', imag_in, table_im, precision=highest)  43 us
  transfers between devices with their start and end apart: 10, of which 10 were waited for; matrix products, arithmetic and copies ran while one was open for 1% of the time, Pallas kernels for 0%

commit v1 on v0

v1 whole, which is shorter than its diff:
```python
import functools

import jax
import jax.numpy as jnp
import ml_dtypes
import numpy as np
from jax import lax
from jax.experimental import pallas as pl
from jax.experimental.pallas import tpu as pltpu
from jax.sharding import PartitionSpec as P

PATCH = 256
HALF = 128
TASKS = 24
BLOCKS = 3
EXT = 768

step_size = 0.1
ridge = 0.5

f32 = jnp.float32
bf16 = jnp.bfloat16


def tables():
    j = np.arange(HALF)
    even = np.exp(-2j * np.pi * (np.outer(j, 2 * j) % PATCH) / PATCH) / 16.0
    odd = np.exp(-2j * np.pi * (np.outer(j, 2 * j + 1) % PATCH) / PATCH) / 16.0

    def left(w):
        return np.block([[w.real, -w.imag], [w.imag, w.real]])

    def split(w):
        high = w.astype(ml_dtypes.bfloat16)
        low = (w - high.astype(np.float64)).astype(ml_dtypes.bfloat16)
        return high, low

    pairs = [split(left(w)) for w in (even, odd)]
    lefts = np.stack([np.stack(pair) for pair in pairs])
    return jnp.asarray(lefts), jnp.asarray(np.swapaxes(lefts, 2, 3).copy())


def shuffle():
    p = np.zeros((PATCH, PATCH), np.float32)
    j = np.arange(HALF)
    p[2 * j, j] = 1
    p[2 * j + 1, HALF + j] = 1
    return p.astype(ml_dtypes.bfloat16)


def two_terms(x):
    high = x.astype(bf16)
    low = (x - high.astype(f32)).astype(bf16)
    return high, low


def right_dot(x, w):
    high, low = two_terms(x)
    both = jnp.concatenate([high, low, high], axis=1)
    return jnp.dot(both, jnp.concatenate([w[0], w[0], w[1]], axis=0), preferred_element_type=f32)


def left_dot(w, x):
    high, low = two_terms(x)
    both = jnp.concatenate([high, low, high], axis=0)
    return jnp.dot(jnp.concatenate([w[0], w[0], w[1]], axis=1), both, preferred_element_type=f32)


def three_dot(x, p):
    high = x.astype(bf16)
    rest = x - high.astype(f32)
    mid = rest.astype(bf16)
    low = (rest - mid.astype(f32)).astype(bf16)
    out = jnp.dot(high, p, preferred_element_type=f32)
    out = out + jnp.dot(mid, p, preferred_element_type=f32)
    return out + jnp.dot(low, p, preferred_element_type=f32)


def prep_kernel(ext_ref, perm_ref, out_ref, even_ref, odd_ref):
    rows = ext_ref.shape[1]
    for c in range(2):
        for b in range(ext_ref.shape[2] // PATCH):
            mixed = three_dot(ext_ref[c, :, b * PATCH : (b + 1) * PATCH], perm_ref[...])
            even_ref[...] = mixed[:, :HALF]
            odd_ref[...] = mixed[:, HALF:]
            for q in range(2):
                out_ref[c, 0, b, q] = even_ref[pl.ds(q, rows // 2, stride=2), :]
                out_ref[c, 1, b, q] = odd_ref[pl.ds(q, rows // 2, stride=2), :]


def prep(ext):
    rows, cols = ext.shape[1:]
    return pl.pallas_call(
        prep_kernel,
        out_shape=jax.ShapeDtypeStruct((2, 2, cols // PATCH, 2, rows // 2, HALF), f32),
        in_specs=[pl.BlockSpec(memory_space=pltpu.VMEM)] * 2,
        out_specs=pl.BlockSpec(memory_space=pltpu.VMEM),
        scratch_shapes=[pltpu.VMEM((rows, HALF), f32)] * 2,
        compiler_params=pltpu.CompilerParams(vmem_limit_bytes=40 << 20),
        cost_estimate=pl.CostEstimate(flops=6 * rows * cols * PATCH * 2, bytes_accessed=16 * rows * cols, transcendentals=0),
    )(ext, jnp.asarray(shuffle()))


def window(pos_ref, t):
    start_y = pos_ref[2 * t] + HALF
    start_x = pos_ref[2 * t + 1] + HALF
    block = jnp.where(start_x >= PATCH, 1, 0)
    offset = start_x - block * PATCH
    rows = [((start_y + q) & 1, (start_y + q) >> 1) for q in range(2)]
    return block, offset, rows


def rolled_probe(probe_ref, offset, p, q):
    source = (p + offset) & 1
    amount = ((offset + source - p) >> 1) & (HALF - 1)
    return [pltpu.roll(probe_ref[c, source, 0, q], amount, 1) for c in range(2)]


def lane_mask(offset, p):
    lane = lax.broadcasted_iota(jnp.int32, (HALF, HALF), 1)
    return lane >= ((offset + 1 - p) >> 1)


def forward_kernel(pos_ref, count_ref, obj_ref, probe_ref, left_ref, right_ref, out_ref):
    t = pl.program_id(0)

    @pl.when(t < count_ref[0])
    def _():
        block, offset, rows = window(pos_ref, t)
        parts = []
        for p in range(2):
            mask = lane_mask(offset, p)
            waves = []
            for q in range(2):
                parity, first = rows[q]
                o = [
                    jnp.where(
                        mask,
                        obj_ref[c, p, block, parity, pl.ds(first, HALF), :],
                        obj_ref[c, p, block + 1, parity, pl.ds(first, HALF), :],
                    )
                    for c in range(2)
                ]
                w = rolled_probe(probe_ref, offset, p, q)
                waves.append(jnp.concatenate([w[0] * o[0] - w[1] * o[1], w[0] * o[1] + w[1] * o[0]], axis=1))
            parts.append(right_dot(jnp.concatenate(waves, axis=0), right_ref[p]))
        low = parts[0] + parts[1]
        high = parts[0] - parts[1]
        sides = []
        for q in range(2):
            r = slice(q * HALF, (q + 1) * HALF)
            re = jnp.concatenate([low[r, :HALF], high[r, :HALF]], axis=1)
            im = jnp.concatenate([low[r, HALF:], high[r, HALF:]], axis=1)
            sides.append(left_dot(left_ref[q], jnp.concatenate([re, im], axis=0)))
        out_ref[0, 0] = sides[0] + sides[1]
        out_ref[0, 1] = sides[0] - sides[1]


def forward(pos, count, obj, probe, lefts, rights):
    whole = pl.BlockSpec(memory_space=pltpu.VMEM)
    return pl.pallas_call(
        forward_kernel,
        out_shape=jax.ShapeDtypeStruct((TASKS, 2, PATCH, PATCH), f32),
        grid_spec=pltpu.PrefetchScalarGridSpec(
            num_scalar_prefetch=2,
            grid=(TASKS,),
            in_specs=[whole] * 4,
            out_specs=pl.BlockSpec((1, 2, PATCH, PATCH), lambda t, pos, count: (t, 0, 0, 0)),
        ),
        compiler_params=pltpu.CompilerParams(vmem_limit_bytes=40 << 20),
        cost_estimate=pl.CostEstimate(flops=TASKS * 24 * PATCH**3, bytes_accessed=TASKS * 8 * PATCH**2, transcendentals=0),
    )(pos, count, obj, probe, lefts, rights)


def inverse_kernel(pos_ref, slot_ref, count_ref, far_ref, frame_ref, probe_ref, left_ref, right_ref, perm_ref, out_ref, acc_ref, even_ref, odd_ref):
    t = pl.program_id(0)

    @pl.when(t == 0)
    def _():
        acc_ref[...] = jnp.zeros_like(acc_ref)

    @pl.when(t < count_ref[0])
    def _():
        block, offset, rows = window(pos_ref, t)
        weighted = []
        for h in range(2):
            re = far_ref[0, h, :HALF, :]
            im = far_ref[0, h, HALF:, :]
            weight = re * re + im * im - frame_ref[0, h * HALF : (h + 1) * HALF, :]
            weighted.append(jnp.concatenate([weight * re, weight * im], axis=0))
        back = [
            left_dot(right_ref[0], weighted[0] + weighted[1]),
            left_dot(right_ref[1], weighted[0] - weighted[1]),
        ]
        low = [jnp.concatenate([b[:HALF, :HALF], b[HALF:, :HALF]], axis=1) for b in back]
        high = [jnp.concatenate([b[:HALF, HALF:], b[HALF:, HALF:]], axis=1) for b in back]
        low = jnp.concatenate(low, axis=0)
        high = jnp.concatenate(high, axis=0)
        chis = [right_dot(low + high, left_ref[0]), right_dot(low - high, left_ref[1])]
        for p in range(2):
            mask = lane_mask(offset, p)
            for q in range(2):
                parity, first = rows[q]
                w = rolled_probe(probe_ref, offset, p, q)
                re = chis[p][q * HALF : (q + 1) * HALF, :HALF]
                im = chis[p][q * HALF : (q + 1) * HALF, HALF:]
                g = [w[0] * re + w[1] * im, w[0] * im - w[1] * re]
                for c in range(2):
                    here = (c, p, block, parity, pl.ds(first, HALF), slice(None))
                    acc_ref[here] = acc_ref[here] + jnp.where(mask, g[c], 0.0)
                    there = (c, p, block + 1, parity, pl.ds(first, HALF), slice(None))
                    acc_ref[there] = acc_ref[there] + jnp.where(mask, 0.0, g[c])

    @pl.when(t == TASKS - 1)
    def _():
        for c in range(2):
            for b in range(BLOCKS):
                for q in range(2):
                    even_ref[pl.ds(q, EXT // 2, stride=2), :] = acc_ref[c, 0, b, q]
                    odd_ref[pl.ds(q, EXT // 2, stride=2), :] = acc_ref[c, 1, b, q]
                mixed = jnp.concatenate([even_ref[...], odd_ref[...]], axis=1)
                out_ref[c, :, b * PATCH : (b + 1) * PATCH] = three_dot(mixed, perm_ref[...])


def inverse(pos, slot, count, far, frames, probe, lefts, rights):
    whole = pl.BlockSpec(memory_space=pltpu.VMEM)
    return pl.pallas_call(
        inverse_kernel,
        out_shape=jax.ShapeDtypeStruct((2, EXT, EXT), f32),
        grid_spec=pltpu.PrefetchScalarGridSpec(
            num_scalar_prefetch=3,
            grid=(TASKS,),
            in_specs=[
                pl.BlockSpec((1, 2, PATCH, PATCH), lambda t, pos, slot, count: (t, 0, 0, 0)),
                pl.BlockSpec((1, PATCH, PATCH), lambda t, pos, slot, count: (slot[t], 0, 0)),
                whole,
                whole,
                whole,
                whole,
            ],
            out_specs=whole,
            scratch_shapes=[
                pltpu.VMEM((2, 2, BLOCKS, 2, EXT // 2, HALF), f32),
                pltpu.VMEM((EXT, HALF), f32),
                pltpu.VMEM((EXT, HALF), f32),
            ],
        ),
        compiler_params=pltpu.CompilerParams(vmem_limit_bytes=40 << 20),
        cost_estimate=pl.CostEstimate(flops=TASKS * 24 * PATCH**3, bytes_accessed=TASKS * 12 * PATCH**2, transcendentals=0),
    )(pos, slot, count, far, frames, probe, lefts, rights, jnp.asarray(shuffle().T.copy()))


def extended_2(block, sides, width):
    for axis, dim in sides:
        count = lax.axis_size(axis)
        forward_pairs = [(i, i + 1) for i in range(count - 1)]
        backward_pairs = [(target, source) for source, target in forward_pairs]
        low = lax.ppermute(lax.slice_in_dim(block, block.shape[dim] - width, None, axis=dim), axis, forward_pairs)
        high = lax.ppermute(lax.slice_in_dim(block, 0, width, axis=dim), axis, backward_pairs)
        block = jnp.concatenate([low, block, high], axis=dim)
    return block


def exchanged(first, last, axis):
    count = lax.axis_size(axis)
    up = [(i, i + 1) for i in range(count - 1)]
    down = [(i + 1, i) for i in range(count - 1)]
    return lax.ppermute(last, axis, up), lax.ppermute(first, axis, down)


def local(extended, probe, arrived, offsets, helper_cols, count):
    task_ids = jnp.arange(TASKS, dtype=jnp.int32)
    same = helper_cols[:, None] == helper_cols[None, :]
    ranks = jnp.sum(jnp.logical_and(same, task_ids[None, :] < task_ids[:, None]), axis=1).astype(jnp.int32)
    slot = helper_cols * 2 + ranks
    lefts, rights = tables()
    obj = prep(extended)
    pro = prep(probe)
    far = forward(offsets, count, obj, pro, lefts, rights)
    return inverse(offsets, slot, count, far, arrived, pro, lefts, rights)


def per_device(object_field, probe, frames, positions, helpers, task_counts):
    arrived = lax.all_to_all(frames[0, 0], "gx", split_axis=0, concat_axis=0, tiled=True)
    extended = extended_2(object_field, (("gx", 2), ("gy", 1)), HALF)
    total = local(
        extended,
        probe,
        arrived.reshape(-1, PATCH, PATCH),
        positions[0, 0].reshape(-1),
        helpers[0, 0, :, 0],
        task_counts[0],
    )

    tile = object_field.shape[1]
    left_in, right_in = exchanged(total[:, :, :HALF], total[:, :, HALF + tile :], "gx")
    middle = total[:, :, HALF : HALF + tile]
    middle = middle.at[:, :, :HALF].add(left_in)
    middle = middle.at[:, :, tile - HALF :].add(right_in)
    up_in, down_in = exchanged(middle[:, :HALF, :], middle[:, HALF + tile :, :], "gy")
    gradient = middle[:, HALF : HALF + tile, :]
    gradient = gradient.at[:, :HALF, :].add(up_in)
    gradient = gradient.at[:, tile - HALF :, :].add(down_in)
    return object_field - step_size * (gradient + ridge * object_field)


def solution(mesh):
    in_specs = (
        P(None, "gy", "gx"),
        P(),
        P("gy", "gx", None, None, None, None),
        P("gy", "gx", None, None),
        P("gy", "gx", None, None),
        P("gy", "gx"),
    )
    out_specs = P(None, "gy", "gx")
    return jax.shard_map(per_device, mesh=mesh, in_specs=in_specs, out_specs=out_specs, check_vma=False)
```

time: 1370 us -> 261 us (0.19); the launches traced: 1350 us -> 262 us
  local copies, waits for them, and re-layouts: 372 us -> 3.91 us
  waiting for transfers between devices: 531 us -> 168 us
  matrix products: 253 us -> 0 us
  other arithmetic: 90.2 us -> 4.74 us
  loops' own time: 62.9 us -> 0 us
  Pallas kernels: 0 us -> 39.6 us
    all_to_all x2 -> x1, waiting for transfers between devices: 484 us -> 0.01 us  [per_device(): lax.all_to_all(frames[0, 0], 'gx', split_axis=0, concat_axis=0, tiled=True)]
    dot_general x12 -> x0, matrix products: 253 us -> none  [the longest x2 55.7 us: left_mul(): jnp.einsum('ij,bjk->bik', table_re + table_im, real_in + imag_in, precisi...]
    dynamic_update_slice x24 -> x0, local copies, waits for them, and re-layouts: 160 us -> none  [add_patch(): lax.dynamic_update_slice(total, current + grads[index], (zero, start_y, s...]
    gather x75 -> x0, local copies, waits for them, and re-layouts: 143 us -> none
    ppermute x4 -> x2, waiting for transfers between devices: 28.7 us -> 140 us  [extended_2(): lax.ppermute(lax.slice_in_dim(block, block.shape[dim] - width, None, axis...]
    another operation x2 -> x0, loops' own time: 62.9 us -> none  [the longest x1 62.9 us: per_device(): lax.fori_loop(0, TASKS, add_patch, jnp.zeros((2, tile + 2 * half, tile +...]
    pallas_call x0 -> x4, Pallas kernels: none -> 39.6 us  [the longest x1 21.8 us: inverse(): pl.pallas_call(inverse_kernel, out_shape=jax.ShapeDtypeStruct((2, EXT, EX...]
    add x25 -> x1, other arithmetic: 37.3 us -> 0.01 us  [local(): slot = helper_cols * 2 + ranks]
  transfers between devices with their start and end apart: 10 -> 9, of which waited for: 10 -> 7; matrix products, arithmetic and copies ran while one was open for 1% -> 2% of each run, Pallas kernels for 0% -> 7%
where the time goes in v1:
time: 261 us; the launch traced here: 262 us
  waiting for transfers between devices  168 us (64%)
  starting transfers between devices  44.4 us (17%)
  Pallas kernels  39.6 us (15%)
  other arithmetic  4.74 us (2%)
  local copies, waits for them, and re-layouts  3.91 us (1%)
    ppermute x2, waiting for transfers between devices, extended_2(): lax.ppermute(lax.slice_in_dim(block, block.shape[dim] - width, None, axis...  140 us
    ppermute x4, starting transfers between devices, exchanged(): return (lax.ppermute(last, axis, up), lax.ppermute(first, axis, down))  25.5 us
    ppermute x4, waiting for transfers between devices, exchanged(): return (lax.ppermute(last, axis, up), lax.ppermute(first, axis, down))  24.1 us
    pallas_call x1, Pallas kernels, inverse(): pl.pallas_call(inverse_kernel, out_shape=jax.ShapeDtypeStruct((2, EXT, EX...  21.8 us
    pallas_call x1, Pallas kernels, forward(): pl.pallas_call(forward_kernel, out_shape=jax.ShapeDtypeStruct((TASKS, 2,...  14.8 us
    ppermute x2, starting transfers between devices, extended_2(): lax.ppermute(lax.slice_in_dim(block, block.shape[dim] - width, None, axis...  7.56 us
    all_to_all x1, starting transfers between devices, per_device(): lax.all_to_all(frames[0, 0], 'gx', split_axis=0, concat_axis=0, tiled=True)  6.85 us
  transfers between devices with their start and end apart: 9, of which 7 were waited for; matrix products, arithmetic and copies ran while one was open for 2% of the time, Pallas kernels for 7%

profile of v1, /device:TPU:91, one launch (start us, length us, event | category | flops | bytes accessed | tf_op | source)
XLA Modules:
  0.0 261.6 jit_solution(10507687337561235796)
XLA Ops:
  0.0 6.8 %all-to-all-start = ((f32[16,2,256,256]{3,2,1,0:T(8,128)}), f32[16,2,256,256]{3,2,1,0:T(8,128)}, u32[]{:S(2)}, u32[]{:S(2)}) async-start(f32[16,2,256,256]{3,2,1,0:T(8,128)} %bitcast.9), calls=%async_computation | async-start | bytes 16777216 | tf_op jit(solution)/shard_map/all_to_all | solution.py:284
  6.9 2.8 %collective-permute-start = (f32[2,512,128]{2,1,0:T(8,128)S(1)}, f32[2,512,128]{2,1,0:T(8,128)S(1)}, u32[]{:S(2)}, u32[]{:S(2)}) collective-permute-start(f32[2,512,128]{2,1,0:T(8,128)S(1)} %get-tuple-element.60), channel_id=1, source_target_pairs={{0,8},{8,16},{16,24},{24,32},{32,40},{40,48},{48,56},{56,64},{64,7... | collective-permute-start | bytes 1572872 | tf_op jit(solution)/shard_map/ppermute | solution.py:258
  9.7 2.5 collective-permute-start.1
  12.2 133.9 %collective-permute-done = f32[2,512,128]{2,1,0:T(8,128)S(1)} collective-permute-done((f32[2,512,128]{2,1,0:T(8,128)S(1)}, f32[2,512,128]{2,1,0:T(8,128)S(1)}, u32[]{:S(2)}, u32[]{:S(2)}) %collective-permute-start) | collective-permute-done | bytes 524320 | tf_op jit(solution)/shard_map/ppermute | solution.py:258
  146.5 1.6 copy-done.7
  148.2 1.0 fusion.7
  149.1 4.8 %collective-permute-start.2 = (f32[2,128,768]{2,1,0:T(8,128)}, f32[2,128,768]{2,1,0:T(8,128)S(1)}, u32[]{:S(2)}, u32[]{:S(2)}) collective-permute-start(f32[2,128,768]{2,1,0:T(8,128)} %get-tuple-element.57), channel_id=1, source_target_pairs={{0,1},{1,2},{2,3},{3,4},{4,5},{5,6},{6,7},{8,9},{9,10},{10,11},{11... | collective-permute-start | bytes 2359304 | tf_op jit(solution)/shard_map/ppermute | solution.py:258
  153.9 1.9 collective-permute-start.3
  156.7 0.4 shard_map.110.probe_ref
  157.3 5.8 %collective-permute-done.2 = f32[2,128,768]{2,1,0:T(8,128)S(1)} collective-permute-done((f32[2,128,768]{2,1,0:T(8,128)}, f32[2,128,768]{2,1,0:T(8,128)S(1)}, u32[]{:S(2)}, u32[]{:S(2)}) %collective-permute-start.2) | collective-permute-done | bytes 786464 | tf_op jit(solution)/shard_map/ppermute | solution.py:258
  163.1 4.1 %collective-permute-done.3 = f32[2,128,768]{2,1,0:T(8,128)S(1)} collective-permute-done((f32[2,128,768]{2,1,0:T(8,128)S(1)}, f32[2,128,768]{2,1,0:T(8,128)S(1)}, u32[]{:S(2)}, u32[]{:S(2)}) %collective-permute-start.3) | collective-permute-done | bytes 786464 | tf_op jit(solution)/shard_map/ppermute | solution.py:259
  167.2 2.2 pad_maximum_fusion.ext_ref
  169.4 2.6 shard_map.109.obj_ref
  172.1 14.8 %shard_map.111.far_ref = f32[24,2,256,256]{3,2,1,0:T(8,128)} custom-call(s32[48]{0:T(128)S(1)} %reshape_squeeze.3.pos_ref, s32[1]{0:T(128)} %bitcast.7.count_ref, f32[2,2,3,2,384,128]{5,4,3,2,1,0:T(8,128)S(1)} %shard_map.109.obj_ref, f32[2,2,1,2,128,128]{5,4,3,2,1,0:T(8,128)S(1)} %shard_map.110.probe_ref, bf16[2,2,256,256]{3,2,1,0:T(8,128)(2,1)S(1)} %copy-done.3, ...), custom_call_target="tpu_custom_call" | custom-call | flops 9663676416 | bytes 12582912 | tf_op jit(solution)/shard_map/pallas_call | solution.py:161
  186.9 21.8 %shard_map.112 = f32[2,768,768]{2,1,0:T(8,128)S(1)} custom-call(s32[48]{0:T(128)S(1)} %reshape_squeeze.3.pos_ref, s32[24]{0:T(128)S(1)} %multiply_add_fusion.slot_ref, s32[1]{0:T(128)} %bitcast.8.count_ref, f32[24,2,256,256]{3,2,1,0:T(8,128)} %shard_map.111.far_ref, f32[32,256,256]{2,1,0:T(8,128)} %bitcast.3.frame_ref, ...), custom_call_target="tpu_custom_call" | custom-call | flops 9663676416 | bytes 18874368 | tf_op jit(solution)/shard_map/pallas_call | solution.py:227
  208.8 1.9 collective-permute-start.4
  210.8 10.2 %collective-permute-start.5 = (f32[2,768,128]{2,1,0:T(8,128)S(1)}, f32[2,768,128]{2,1,0:T(8,128)S(1)}, u32[]{:S(2)}, u32[]{:S(2)}) collective-permute-start(f32[2,768,128]{2,1,0:T(8,128)S(1)} %get-tuple-element.53), channel_id=1, source_target_pairs={{8,0},{16,8},{24,16},{32,24},{40,32},{48,40},{56,48},{64,56},{72,6... | collective-permute-start | bytes 2359304 | tf_op jit(solution)/shard_map/ppermute | solution.py:268
  221.4 15.0 %collective-permute-done.4 = f32[2,768,128]{2,1,0:T(8,128)S(1)} collective-permute-done((f32[2,768,128]{2,1,0:T(8,128)S(1)}, f32[2,768,128]{2,1,0:T(8,128)S(1)}, u32[]{:S(2)}, u32[]{:S(2)}) %collective-permute-start.4) | collective-permute-done | bytes 786464 | tf_op jit(solution)/shard_map/ppermute | solution.py:268
  236.6 0.8 collective-permute-done.5
  237.6 11.3 %collective-permute-start.6 = (f32[2,128,512]{2,1,0:T(8,128)S(1)}, f32[2,128,512]{2,1,0:T(8,128)S(1)}, u32[]{:S(2)}, u32[]{:S(2)}) collective-permute-start(f32[2,128,512]{2,1,0:T(8,128)S(1)} %get-tuple-element.56), channel_id=1, source_target_pairs={{0,1},{1,2},{2,3},{3,4},{4,5},{5,6},{6,7},{8,9},{9,10},{10,11},{11... | collective-permute-start | bytes 1572872 | tf_op jit(solution)/shard_map/ppermute | solution.py:268
  248.9 2.1 collective-permute-start.7
  251.2 3.9 %collective-permute-done.6 = f32[2,128,512]{2,1,0:T(8,128)S(1)} collective-permute-done((f32[2,128,512]{2,1,0:T(8,128)S(1)}, f32[2,128,512]{2,1,0:T(8,128)S(1)}, u32[]{:S(2)}, u32[]{:S(2)}) %collective-permute-start.6) | collective-permute-done | bytes 524320 | tf_op jit(solution)/shard_map/ppermute | solution.py:268
  255.1 4.5 %collective-permute-done.7 = f32[2,128,512]{2,1,0:T(8,128)S(1)} collective-permute-done((f32[2,128,512]{2,1,0:T(8,128)S(1)}, f32[2,128,512]{2,1,0:T(8,128)S(1)}, u32[]{:S(2)}, u32[]{:S(2)}) %collective-permute-start.7) | collective-permute-done | bytes 524320 | tf_op jit(solution)/shard_map/ppermute | solution.py:268
  259.7 1.8 multiply_subtract_fusion
  (37 shorter events, 2.0 us)
Async XLA Ops:
  0.0 6.8 %copy-start.5 = (f32[2,512,512]{2,1,0:T(8,128)S(1)}, f32[2,512,512]{2,1,0:T(8,128)}, u32[]{:S(2)}) copy-start(f32[2,512,512]{2,1,0:T(8,128)} %param.19) | copy-start | bytes 6291460
  0.0 186.9 %all-to-all-start = ((f32[16,2,256,256]{3,2,1,0:T(8,128)}), f32[16,2,256,256]{3,2,1,0:T(8,128)}, u32[]{:S(2)}, u32[]{:S(2)}) async-start(f32[16,2,256,256]{3,2,1,0:T(8,128)} %bitcast.9), calls=%async_computation | async-start | bytes 16777216 | tf_op jit(solution)/shard_map/all_to_all | solution.py:284
  6.9 139.2 %collective-permute-start = (f32[2,512,128]{2,1,0:T(8,128)S(1)}, f32[2,512,128]{2,1,0:T(8,128)S(1)}, u32[]{:S(2)}, u32[]{:S(2)}) collective-permute-start(f32[2,512,128]{2,1,0:T(8,128)S(1)} %get-tuple-element.60), channel_id=1, source_target_pairs={{0,8},{8,16},{16,24},{24,32},{32,40},{40,48},{48,56},{56,64},{64,7... | collective-permute-start | bytes 1572872 | tf_op jit(solution)/shard_map/ppermute | solution.py:258
  9.7 136.7 %collective-permute-start.1 = (f32[2,512,128]{2,1,0:T(8,128)S(1)}, f32[2,512,128]{2,1,0:T(8,128)S(1)}, u32[]{:S(2)}, u32[]{:S(2)}) collective-permute-start(f32[2,512,128]{2,1,0:T(8,128)S(1)} %get-tuple-element.59), channel_id=1, source_target_pairs={{8,0},{16,8},{24,16},{32,24},{40,32},{48,40},{56,48},{64,56},{72,6... | collective-permute-start | bytes 1572872 | tf_op jit(solution)/shard_map/ppermute | solution.py:259
  146.4 10.1 %copy-start.8 = (s32[1,1,24,2]{2,3,1,0:T(2,128)S(1)}, s32[1,1,24,2]{2,3,1,0:T(2,128)}, u32[]{:S(2)}) copy-start(s32[1,1,24,2]{2,3,1,0:T(2,128)} %param.22) | copy-start | bytes 580
  146.4 10.3 %copy-start = (bf16[256,256]{1,0:T(8,128)(2,1)S(1)}, bf16[256,256]{1,0:T(8,128)(2,1)}, u32[]{:S(2)}) copy-start(bf16[256,256]{1,0:T(8,128)(2,1)} %constant.123.clone.perm_ref) | copy-start | bytes 393220
  146.4 10.3 %copy-start.1 = (f32[2,256,256]{2,1,0:T(8,128)S(1)}, f32[2,256,256]{2,1,0:T(8,128)}, u32[]{:S(2)}) copy-start(f32[2,256,256]{2,1,0:T(8,128)} %ext_ref.1) | copy-start | bytes 1572868
  146.4 10.7 %copy-start.9 = (s32[1,1,24,1]{2,3,1,0:T(1,128)S(1)}, s32[1,1,24,1]{2,3,1,0:T(1,128)}, u32[]{:S(2)}) copy-start(s32[1,1,24,1]{2,3,1,0:T(1,128)} %param.23) | copy-start | bytes 292
  146.5 1.7 copy-start.7
  149.1 14.0 %collective-permute-start.2 = (f32[2,128,768]{2,1,0:T(8,128)}, f32[2,128,768]{2,1,0:T(8,128)S(1)}, u32[]{:S(2)}, u32[]{:S(2)}) collective-permute-start(f32[2,128,768]{2,1,0:T(8,128)} %get-tuple-element.57), channel_id=1, source_target_pairs={{0,1},{1,2},{2,3},{3,4},{4,5},{5,6},{6,7},{8,9},{9,10},{10,11},{11... | collective-permute-start | bytes 2359304 | tf_op jit(solution)/shard_map/ppermute | solution.py:258
  153.9 13.3 %collective-permute-start.3 = (f32[2,128,768]{2,1,0:T(8,128)S(1)}, f32[2,128,768]{2,1,0:T(8,128)S(1)}, u32[]{:S(2)}, u32[]{:S(2)}) collective-permute-start(f32[2,128,768]{2,1,0:T(8,128)S(1)} %get-tuple-element.58), channel_id=1, source_target_pairs={{1,0},{2,1},{3,2},{4,3},{5,4},{6,5},{7,6},{9,8},{10,9},{11,10},{12... | collective-permute-start | bytes 2359304 | tf_op jit(solution)/shard_map/ppermute | solution.py:259
  169.4 2.6 %copy-start.2 = (bf16[2,2,256,256]{3,2,1,0:T(8,128)(2,1)S(1)}, bf16[2,2,256,256]{3,2,1,0:T(8,128)(2,1)}, u32[]{:S(2)}) copy-start(bf16[2,2,256,256]{3,2,1,0:T(8,128)(2,1)} %constant.122.clone.right_ref) | copy-start | bytes 1572868
  169.4 2.6 %copy-start.3 = (bf16[2,2,256,256]{3,2,1,0:T(8,128)(2,1)S(1)}, bf16[2,2,256,256]{3,2,1,0:T(8,128)(2,1)}, u32[]{:S(2)}) copy-start(bf16[2,2,256,256]{3,2,1,0:T(8,128)(2,1)} %constant.121.clone.left_ref) | copy-start | bytes 1572868
  172.1 14.8 %copy-start.4 = (bf16[256,256]{1,0:T(8,128)(2,1)S(1)}, bf16[256,256]{1,0:T(8,128)(2,1)}, u32[]{:S(2)}) copy-start(bf16[256,256]{1,0:T(8,128)(2,1)} %constant.124.clone.perm_ref) | copy-start | bytes 393220
  208.8 27.6 %collective-permute-start.4 = (f32[2,768,128]{2,1,0:T(8,128)S(1)}, f32[2,768,128]{2,1,0:T(8,128)S(1)}, u32[]{:S(2)}, u32[]{:S(2)}) collective-permute-start(f32[2,768,128]{2,1,0:T(8,128)S(1)} %get-tuple-element.54), channel_id=1, source_target_pairs={{0,8},{8,16},{16,24},{24,32},{32,40},{40,48},{48,56},{56,64},{64,7... | collective-permute-start | bytes 2359304 | tf_op jit(solution)/shard_map/ppermute | solution.py:268
  210.8 26.6 %collective-permute-start.5 = (f32[2,768,128]{2,1,0:T(8,128)S(1)}, f32[2,768,128]{2,1,0:T(8,128)S(1)}, u32[]{:S(2)}, u32[]{:S(2)}) collective-permute-start(f32[2,768,128]{2,1,0:T(8,128)S(1)} %get-tuple-element.53), channel_id=1, source_target_pairs={{8,0},{16,8},{24,16},{32,24},{40,32},{48,40},{56,48},{64,56},{72,6... | collective-permute-start | bytes 2359304 | tf_op jit(solution)/shard_map/ppermute | solution.py:268
  237.6 17.4 %collective-permute-start.6 = (f32[2,128,512]{2,1,0:T(8,128)S(1)}, f32[2,128,512]{2,1,0:T(8,128)S(1)}, u32[]{:S(2)}, u32[]{:S(2)}) collective-permute-start(f32[2,128,512]{2,1,0:T(8,128)S(1)} %get-tuple-element.56), channel_id=1, source_target_pairs={{0,1},{1,2},{2,3},{3,4},{4,5},{5,6},{6,7},{8,9},{9,10},{10,11},{11... | collective-permute-start | bytes 1572872 | tf_op jit(solution)/shard_map/ppermute | solution.py:268
  248.9 10.8 %copy-start.6 = (f32[2,512,512]{2,1,0:T(8,128)S(1)}, f32[2,512,512]{2,1,0:T(8,128)}, u32[]{:S(2)}) copy-start(f32[2,512,512]{2,1,0:T(8,128)} %param.19) | copy-start | bytes 6291460
  248.9 10.6 %collective-permute-start.7 = (f32[2,128,512]{2,1,0:T(8,128)S(1)}, f32[2,128,512]{2,1,0:T(8,128)S(1)}, u32[]{:S(2)}, u32[]{:S(2)}) collective-permute-start(f32[2,128,512]{2,1,0:T(8,128)S(1)} %get-tuple-element.55), channel_id=1, source_target_pairs={{1,0},{2,1},{3,2},{4,3},{5,4},{6,5},{7,6},{9,8},{10,9},{11,10},{12... | collective-permute-start | bytes 1572872 | tf_op jit(solution)/shard_map/ppermute | solution.py:268

commit v2 on v1

--- a/solution.py
+++ b/solution.py
@@ -8,6 +8,7 @@
 from jax.experimental import pallas as pl
 from jax.experimental.pallas import tpu as pltpu
 from jax.sharding import PartitionSpec as P
+
 
 PATCH = 256
 HALF = 128
@@ -172,16 +173,23 @@
     )(pos, count, obj, probe, lefts, rights)
 
 
-def inverse_kernel(pos_ref, slot_ref, count_ref, far_ref, frame_ref, probe_ref, left_ref, right_ref, perm_ref, out_ref, acc_ref, even_ref, odd_ref):
-    t = pl.program_id(0)
-
-    @pl.when(t == 0)
+def inverse_kernel(last, pos_ref, order_ref, slot_ref, count_ref, far_ref, frame_ref, probe_ref, left_ref, right_ref, *rest):
+    if last:
+        perm_ref, before_ref, out_ref, acc_ref, even_ref, odd_ref = rest
+    else:
+        (acc_ref,) = rest
+    i = pl.program_id(0)
+
+    @pl.when(i == 0)
     def _():
-        acc_ref[...] = jnp.zeros_like(acc_ref)
-
-    @pl.when(t < count_ref[0])
+        if last:
+            acc_ref[...] = before_ref[...]
+        else:
+            acc_ref[...] = jnp.zeros_like(acc_ref)
+
+    @pl.when(i < count_ref[0])
     def _():
-        block, offset, rows = window(pos_ref, t)
+        block, offset, rows = window(pos_ref, order_ref[i])
         weighted = []
         for h in range(2):
             re = far_ref[0, h, :HALF, :]
@@ -211,43 +219,41 @@
                     there = (c, p, block + 1, parity, pl.ds(first, HALF), slice(None))
                     acc_ref[there] = acc_ref[there] + jnp.where(mask, 0.0, g[c])
 
-    @pl.when(t == TASKS - 1)
-    def _():
-        for c in range(2):
-            for b in range(BLOCKS):
-                for q in range(2):
-                    even_ref[pl.ds(q, EXT // 2, stride=2), :] = acc_ref[c, 0, b, q]
-                    odd_ref[pl.ds(q, EXT // 2, stride=2), :] = acc_ref[c, 1, b, q]
-                mixed = jnp.concatenate([even_ref[...], odd_ref[...]], axis=1)
-                out_ref[c, :, b * PATCH : (b + 1) * PATCH] = three_dot(mixed, perm_ref[...])
-
-
-def inverse(pos, slot, count, far, frames, probe, lefts, rights):
+    if last:
+
+        @pl.when(i == pl.num_programs(0) - 1)
+        def _():
+            for c in range(2):
+                for b in range(BLOCKS):
+                    for q in range(2):
+                        even_ref[pl.ds(q, EXT // 2, stride=2), :] = acc_ref[c, 0, b, q]
+                        odd_ref[pl.ds(q, EXT // 2, stride=2), :] = acc_ref[c, 1, b, q]
+                    mixed = jnp.concatenate([even_ref[...], odd_ref[...]], axis=1)
+                    out_ref[c, :, b * PATCH : (b + 1) * PATCH] = three_dot(mixed, perm_ref[...])
+
+
+def inverse(last, most, pos, order, slot, count, far, frames, probe, lefts, rights, before=None):
     whole = pl.BlockSpec(memory_space=pltpu.VMEM)
+    parts = (2, 2, BLOCKS, 2, EXT // 2, HALF)
+    more = (jnp.asarray(shuffle().T.copy()), before) if last else ()
+    strips = [pltpu.VMEM(parts, f32)] + [pltpu.VMEM((EXT, HALF), f32)] * 2
     return pl.pallas_call(
-        inverse_kernel,
-        out_shape=jax.ShapeDtypeStruct((2, EXT, EXT), f32),
+        functools.partial(inverse_kernel, last),
+        out_shape=jax.ShapeDtypeStruct((2, EXT, EXT) if last else parts, f32),
         grid_spec=pltpu.PrefetchScalarGridSpec(
-            num_scalar_prefetch=3,
-            grid=(TASKS,),
+            num_scalar_prefetch=4,
+            grid=(most,),
             in_specs=[
-                pl.BlockSpec((1, 2, PATCH, PATCH), lambda t, pos, slot, count: (t, 0, 0, 0)),
-                pl.BlockSpec((1, PATCH, PATCH), lambda t, pos, slot, count: (slot[t], 0, 0)),
-                whole,
-                whole,
-                whole,
-                whole,
-            ],
+                pl.BlockSpec((1, 2, PATCH, PATCH), lambda i, pos, order, slot, count: (order[i], 0, 0, 0)),
+                pl.BlockSpec((1, PATCH, PATCH), lambda i, pos, order, slot, count: (slot[i], 0, 0)),
+            ]
+            + [whole] * (3 + len(more)),
             out_specs=whole,
-            scratch_shapes=[
-                pltpu.VMEM((2, 2, BLOCKS, 2, EXT // 2, HALF), f32),
-                pltpu.VMEM((EXT, HALF), f32),
-                pltpu.VMEM((EXT, HALF), f32),
-            ],
+            scratch_shapes=strips if last else [],
         ),
         compiler_params=pltpu.CompilerParams(vmem_limit_bytes=40 << 20),
-        cost_estimate=pl.CostEstimate(flops=TASKS * 24 * PATCH**3, bytes_accessed=TASKS * 12 * PATCH**2, transcendentals=0),
-    )(pos, slot, count, far, frames, probe, lefts, rights, jnp.asarray(shuffle().T.copy()))
+        cost_estimate=pl.CostEstimate(flops=most * 24 * PATCH**3, bytes_accessed=most * 12 * PATCH**2, transcendentals=0),
+    )(pos, order, slot, count, far, frames, probe, lefts, rights, *more)
 
 
 def extended_2(block, sides, width):
@@ -268,25 +274,41 @@
     return lax.ppermute(last, axis, up), lax.ppermute(first, axis, down)
 
 
-def local(extended, probe, arrived, offsets, helper_cols, count):
+def ordered(chosen, helper_cols, most):
+    task_ids = jnp.arange(TASKS, dtype=jnp.int32)
+    place = jnp.sum(jnp.logical_and(chosen[None, :], task_ids[None, :] < task_ids[:, None]), axis=1)
+    spot = jnp.logical_and(chosen[None, :], place[None, :] == jnp.arange(most)[:, None])
+    order = jnp.sum(jnp.where(spot, task_ids[None, :], 0), axis=1).astype(jnp.int32)
+    slot = jnp.sum(jnp.where(spot, helper_cols[None, :], 0), axis=1).astype(jnp.int32)
+    return order, slot, jnp.sum(chosen).astype(jnp.int32).reshape(1)
+
+
+def local(extended, probe, arrived_0, arrived_1, offsets, helper_cols, count):
     task_ids = jnp.arange(TASKS, dtype=jnp.int32)
     same = helper_cols[:, None] == helper_cols[None, :]
-    ranks = jnp.sum(jnp.logical_and(same, task_ids[None, :] < task_ids[:, None]), axis=1).astype(jnp.int32)
-    slot = helper_cols * 2 + ranks
+    second = jnp.any(jnp.logical_and(same, task_ids[None, :] < task_ids[:, None]), axis=1)
+    valid = task_ids < count[0]
+    order_0 = ordered(jnp.logical_and(valid, jnp.logical_not(second)), helper_cols, 16)
+    order_1 = ordered(jnp.logical_and(valid, second), helper_cols, TASKS // 2)
     lefts, rights = tables()
     obj = prep(extended)
     pro = prep(probe)
     far = forward(offsets, count, obj, pro, lefts, rights)
-    return inverse(offsets, slot, count, far, arrived, pro, lefts, rights)
+    part = inverse(False, 16, offsets, *order_0, far, arrived_0, pro, lefts, rights)
+    return inverse(True, TASKS // 2, offsets, *order_1, far, arrived_1, pro, lefts, rights, part)
 
 
 def per_device(object_field, probe, frames, positions, helpers, task_counts):
-    arrived = lax.all_to_all(frames[0, 0], "gx", split_axis=0, concat_axis=0, tiled=True)
-    extended = extended_2(object_field, (("gx", 2), ("gy", 1)), HALF)
+    extended = extended_2(object_field, (("gx", 2),), HALF)
+    kept = frames[0, 0]
+    arrived = lax.all_to_all(kept[:, 0], "gx", split_axis=0, concat_axis=0, tiled=True)
+    arrived_1 = lax.all_to_all(kept[:, 1], "gx", split_axis=0, concat_axis=0, tiled=True)
+    extended = extended_2(extended, (("gy", 1),), HALF)
     total = local(
         extended,
         probe,
-        arrived.reshape(-1, PATCH, PATCH),
+        arrived,
+        arrived_1,
         positions[0, 0].reshape(-1),
         helpers[0, 0, :, 0],
         task_counts[0],

time: 261 us -> 260 us (level)
  the two profiles are of different devices: /device:TPU:91 before, /device:TPU:65 now
where the time goes in v2:
time: 260 us; the launch traced here: 259 us
  waiting for transfers between devices  85.8 us (33%)
  blocking collectives  55 us (21%)
  starting transfers between devices  54.6 us (21%)
  Pallas kernels  44.1 us (17%)
  local copies, waits for them, and re-layouts  12.5 us (5%)
  other arithmetic  5.75 us (2%)
    ppermute x2, waiting for transfers between devices, extended_2(): lax.ppermute(lax.slice_in_dim(block, block.shape[dim] - width, None, axis...  63 us
    all_to_all x1, blocking collectives, per_device(): lax.all_to_all(kept[:, 0], 'gx', split_axis=0, concat_axis=0, tiled=True)  55 us
    ppermute x4, starting transfers between devices, exchanged(): return (lax.ppermute(last, axis, up), lax.ppermute(first, axis, down))  33.2 us
    pallas_call x2, Pallas kernels, inverse(): pl.pallas_call(functools.partial(inverse_kernel, last), out_shape=jax.Sha...  23.4 us
    pallas_call x1, Pallas kernels, forward(): pl.pallas_call(forward_kernel, out_shape=jax.ShapeDtypeStruct((TASKS, 2,...  17.6 us
    ppermute x4, waiting for transfers between devices, exchanged(): return (lax.ppermute(last, axis, up), lax.ppermute(first, axis, down))  16.7 us
    ppermute x2, starting transfers between devices, extended_2(): lax.ppermute(lax.slice_in_dim(block, block.shape[dim] - width, None, axis...  8.97 us
    unnamed x28, local copies, waits for them, and re-layouts  7.99 us
  transfers between devices with their start and end apart: 9, of which 8 were waited for; matrix products, arithmetic and copies ran while one was open for 2% of the time, Pallas kernels for 13%

profile of v2, /device:TPU:65, one launch (start us, length us, event | category | flops | bytes accessed | tf_op | source)
XLA Modules:
  0.0 258.7 jit_solution(4169410096260566610)
XLA Ops:
  0.0 3.9 %copy.19 = f32[1,1,16,2,256,256]{5,4,2,3,1,0:T(8,128)S(1)} copy(f32[1,1,16,2,256,256]{5,4,3,2,1,0:T(8,128)} %param.21) | data formatting | bytes 16777216 | tf_op args[2]
  3.9 2.6 %slice_bitcast_fusion = (f32[16,256,256]{2,1,0:T(8,128)S(1)}, f32[16,256,256]{2,1,0:T(8,128)}) fusion(f32[16,2,256,256]{3,2,0,1:T(8,128)S(1)} %bitcast.16), kind=kLoop, calls=%fused_computation.2 | loop fusion | bytes 16777216 | tf_op jit(solution)/shard_map/squeeze | solution.py:304
  6.5 55.0 %all_to_all.10.frame_ref = f32[16,256,256]{2,1,0:T(8,128)} all-to-all(f32[16,256,256]{2,1,0:T(8,128)S(1)} %get-tuple-element.61), channel_id=1, replica_groups=mesh['gx'=16,'gy'=8] {'gx'}, dimensions={0} | all-to-all | bytes 8388608 | tf_op jit(solution)/shard_map/all_to_all | solution.py:304
  61.5 6.3 %all-to-all-start = ((f32[16,256,256]{2,1,0:T(8,128)}), f32[16,256,256]{2,1,0:T(8,128)}, u32[]{:S(2)}, u32[]{:S(2)}) async-start(f32[16,256,256]{2,1,0:T(8,128)} %get-tuple-element.62), calls=%async_computation | async-start | bytes 8388608 | tf_op jit(solution)/shard_map/all_to_all | solution.py:305
  67.9 3.1 %collective-permute-start = (f32[2,512,128]{2,1,0:T(8,128)S(1)}, f32[2,512,128]{2,1,0:T(8,128)S(1)}, u32[]{:S(2)}, u32[]{:S(2)}) collective-permute-start(f32[2,512,128]{2,1,0:T(8,128)S(1)} %get-tuple-element.70), channel_id=1, source_target_pairs={{0,8},{8,16},{16,24},{24,32},{32,40},{40,48},{48,56},{56,64},{64,7... | collective-permute-start | bytes 1572872 | tf_op jit(solution)/shard_map/ppermute | solution.py:264
  71.0 4.3 %collective-permute-start.1 = (f32[2,512,128]{2,1,0:T(8,128)S(1)}, f32[2,512,128]{2,1,0:T(8,128)S(1)}, u32[]{:S(2)}, u32[]{:S(2)}) collective-permute-start(f32[2,512,128]{2,1,0:T(8,128)S(1)} %get-tuple-element.69), channel_id=1, source_target_pairs={{8,0},{16,8},{24,16},{32,24},{40,32},{48,40},{56,48},{64,56},{72,6... | collective-permute-start | bytes 1572872 | tf_op jit(solution)/shard_map/ppermute | solution.py:265
  75.3 58.2 %collective-permute-done = f32[2,512,128]{2,1,0:T(8,128)S(1)} collective-permute-done((f32[2,512,128]{2,1,0:T(8,128)S(1)}, f32[2,512,128]{2,1,0:T(8,128)S(1)}, u32[]{:S(2)}, u32[]{:S(2)}) %collective-permute-start) | collective-permute-done | bytes 524320 | tf_op jit(solution)/shard_map/ppermute | solution.py:264
  133.7 2.1 collective-permute-done.1
  138.4 5.9 %collective-permute-start.2 = (f32[2,128,768]{2,1,0:T(8,128)}, f32[2,128,768]{2,1,0:T(8,128)S(1)}, u32[]{:S(2)}, u32[]{:S(2)}) collective-permute-start(f32[2,128,768]{2,1,0:T(8,128)} %get-tuple-element.67), channel_id=1, source_target_pairs={{0,1},{1,2},{2,3},{3,4},{4,5},{5,6},{6,7},{8,9},{9,10},{10,11},{11... | collective-permute-start | bytes 2359304 | tf_op jit(solution)/shard_map/ppermute | solution.py:264
  144.3 1.9 collective-permute-start.3
  148.8 4.8 %collective-permute-done.2 = f32[2,128,768]{2,1,0:T(8,128)S(1)} collective-permute-done((f32[2,128,768]{2,1,0:T(8,128)}, f32[2,128,768]{2,1,0:T(8,128)S(1)}, u32[]{:S(2)}, u32[]{:S(2)}) %collective-permute-start.2) | collective-permute-done | bytes 786464 | tf_op jit(solution)/shard_map/ppermute | solution.py:264
  153.6 4.1 %collective-permute-done.3 = f32[2,128,768]{2,1,0:T(8,128)S(1)} collective-permute-done((f32[2,128,768]{2,1,0:T(8,128)S(1)}, f32[2,128,768]{2,1,0:T(8,128)S(1)}, u32[]{:S(2)}, u32[]{:S(2)}) %collective-permute-start.3) | collective-permute-done | bytes 786464 | tf_op jit(solution)/shard_map/ppermute | solution.py:265
  157.6 2.2 pad_maximum_fusion.ext_ref
  159.9 2.7 %shard_map.109.obj_ref = f32[2,2,3,2,384,128]{5,4,3,2,1,0:T(8,128)S(1)} custom-call(f32[2,768,768]{2,1,0:T(8,128)S(1)} %pad_maximum_fusion.ext_ref, bf16[256,256]{1,0:T(8,128)(2,1)S(1)} %copy-done.2), custom_call_target="tpu_custom_call" | custom-call | flops 1811939328 | bytes 9437184 | tf_op jit(solution)/shard_map/pallas_call | solution.py:94
  162.5 17.6 %shard_map.111.far_ref = f32[24,2,256,256]{3,2,1,0:T(8,128)} custom-call(s32[48]{0:T(128)S(1)} %reshape_squeeze.3.pos_ref, s32[1]{0:T(128)} %bitcast.15.count_ref, f32[2,2,3,2,384,128]{5,4,3,2,1,0:T(8,128)S(1)} %shard_map.109.obj_ref, f32[2,2,1,2,128,128]{5,4,3,2,1,0:T(8,128)S(1)} %shard_map.110.probe_ref, bf16[2,2,256,256]{3,2,1,0:T(8,128)(2,1)S(1)} %copy-done.4, ...), custom_call_target="tpu_custom_call" | custom-call | flops 9663676416 | bytes 12582912 | tf_op jit(solution)/shard_map/pallas_call | solution.py:162
  180.1 13.3 %shard_map.112.rest_1_ = f32[2,2,3,2,384,128]{5,4,3,2,1,0:T(8,128)S(1)} custom-call(s32[48]{0:T(128)S(1)} %reshape_squeeze.3.pos_ref, s32[16]{0:T(128)S(1)} %get-tuple-element.54.order_ref, s32[16]{0:T(128)S(1)} %get-tuple-element.53.slot_ref, s32[1]{0:T(128)} %bitcast.6.count_ref, f32[24,2,256,256]{3,2,1,0:T(8,128)} %shard_map.111.far_ref, ...), custom_call_target="tpu_custom_call" | custom-call | flops 6442450944 | bytes 12582912 | tf_op jit(solution)/shard_map/pallas_call | solution.py:240
  193.4 2.1 copy-done
  195.5 10.1 %shard_map.113 = f32[2,768,768]{2,1,0:T(8,128)S(1)} custom-call(s32[48]{0:T(128)S(1)} %reshape_squeeze.3.pos_ref, s32[12]{0:T(128)S(1)} %get-tuple-element.56.order_ref, s32[12]{0:T(128)S(1)} %get-tuple-element.55.slot_ref, s32[1]{0:T(128)} %bitcast.2.count_ref, f32[24,2,256,256]{3,2,1,0:T(8,128)} %shard_map.111.far_ref, ...), custom_call_target="tpu_custom_call" | custom-call | flops 4831838208 | bytes 9437184 | tf_op jit(solution)/shard_map/pallas_call | solution.py:240
  207.7 15.3 %collective-permute-start.5 = (f32[2,768,128]{2,1,0:T(8,128)S(1)}, f32[2,768,128]{2,1,0:T(8,128)S(1)}, u32[]{:S(2)}, u32[]{:S(2)}) collective-permute-start(f32[2,768,128]{2,1,0:T(8,128)S(1)} %get-tuple-element.63), channel_id=1, source_target_pairs={{8,0},{16,8},{24,16},{32,24},{40,32},{48,40},{56,48},{64,56},{72,6... | collective-permute-start | bytes 2359304 | tf_op jit(solution)/shard_map/ppermute | solution.py:274
  223.4 7.0 %collective-permute-done.4 = f32[2,768,128]{2,1,0:T(8,128)S(1)} collective-permute-done((f32[2,768,128]{2,1,0:T(8,128)S(1)}, f32[2,768,128]{2,1,0:T(8,128)S(1)}, u32[]{:S(2)}, u32[]{:S(2)}) %collective-permute-start.4) | collective-permute-done | bytes 786464 | tf_op jit(solution)/shard_map/ppermute | solution.py:274
  232.2 13.9 %collective-permute-start.6 = (f32[2,128,512]{2,1,0:T(8,128)S(1)}, f32[2,128,512]{2,1,0:T(8,128)S(1)}, u32[]{:S(2)}, u32[]{:S(2)}) collective-permute-start(f32[2,128,512]{2,1,0:T(8,128)S(1)} %get-tuple-element.66), channel_id=1, source_target_pairs={{0,1},{1,2},{2,3},{3,4},{4,5},{5,6},{6,7},{8,9},{9,10},{10,11},{11... | collective-permute-start | bytes 1572872 | tf_op jit(solution)/shard_map/ppermute | solution.py:274
  246.1 2.1 collective-permute-start.7
  248.3 3.9 %collective-permute-done.6 = f32[2,128,512]{2,1,0:T(8,128)S(1)} collective-permute-done((f32[2,128,512]{2,1,0:T(8,128)S(1)}, f32[2,128,512]{2,1,0:T(8,128)S(1)}, u32[]{:S(2)}, u32[]{:S(2)}) %collective-permute-start.6) | collective-permute-done | bytes 524320 | tf_op jit(solution)/shard_map/ppermute | solution.py:274
  252.2 4.5 %collective-permute-done.7 = f32[2,128,512]{2,1,0:T(8,128)S(1)} collective-permute-done((f32[2,128,512]{2,1,0:T(8,128)S(1)}, f32[2,128,512]{2,1,0:T(8,128)S(1)}, u32[]{:S(2)}, u32[]{:S(2)}) %collective-permute-start.7) | collective-permute-done | bytes 524320 | tf_op jit(solution)/shard_map/ppermute | solution.py:274
  (48 shorter events, 11.2 us)
Async XLA Ops:
  61.5 6.3 %copy-start.7 = (f32[2,512,512]{2,1,0:T(8,128)S(1)}, f32[2,512,512]{2,1,0:T(8,128)}, u32[]{:S(2)}) copy-start(f32[2,512,512]{2,1,0:T(8,128)} %param.19) | copy-start | bytes 6291460
  61.5 134.0 %all-to-all-start = ((f32[16,256,256]{2,1,0:T(8,128)}), f32[16,256,256]{2,1,0:T(8,128)}, u32[]{:S(2)}, u32[]{:S(2)}) async-start(f32[16,256,256]{2,1,0:T(8,128)} %get-tuple-element.62), calls=%async_computation | async-start | bytes 8388608 | tf_op jit(solution)/shard_map/all_to_all | solution.py:305
  67.9 65.6 %collective-permute-start = (f32[2,512,128]{2,1,0:T(8,128)S(1)}, f32[2,512,128]{2,1,0:T(8,128)S(1)}, u32[]{:S(2)}, u32[]{:S(2)}) collective-permute-start(f32[2,512,128]{2,1,0:T(8,128)S(1)} %get-tuple-element.70), channel_id=1, source_target_pairs={{0,8},{8,16},{16,24},{24,32},{32,40},{40,48},{48,56},{56,64},{64,7... | collective-permute-start | bytes 1572872 | tf_op jit(solution)/shard_map/ppermute | solution.py:264
  71.0 64.8 %collective-permute-start.1 = (f32[2,512,128]{2,1,0:T(8,128)S(1)}, f32[2,512,128]{2,1,0:T(8,128)S(1)}, u32[]{:S(2)}, u32[]{:S(2)}) collective-permute-start(f32[2,512,128]{2,1,0:T(8,128)S(1)} %get-tuple-element.69), channel_id=1, source_target_pairs={{8,0},{16,8},{24,16},{32,24},{40,32},{48,40},{56,48},{64,56},{72,6... | collective-permute-start | bytes 1572872 | tf_op jit(solution)/shard_map/ppermute | solution.py:265
  133.7 13.2 %copy-start.11 = (s32[1,1,24,2]{2,3,1,0:T(2,128)S(1)}, s32[1,1,24,2]{2,3,1,0:T(2,128)}, u32[]{:S(2)}) copy-start(s32[1,1,24,2]{2,3,1,0:T(2,128)} %param.22) | copy-start | bytes 580
  133.7 13.4 %copy-start.2 = (bf16[256,256]{1,0:T(8,128)(2,1)S(1)}, bf16[256,256]{1,0:T(8,128)(2,1)}, u32[]{:S(2)}) copy-start(bf16[256,256]{1,0:T(8,128)(2,1)} %constant.123.clone.perm_ref) | copy-start | bytes 393220
  133.7 13.4 %copy-start.5 = (f32[2,256,256]{2,1,0:T(8,128)S(1)}, f32[2,256,256]{2,1,0:T(8,128)}, u32[]{:S(2)}) copy-start(f32[2,256,256]{2,1,0:T(8,128)} %ext_ref.1) | copy-start | bytes 1572868
  133.7 13.8 %copy-start.10 = (s32[1,1,24,1]{2,3,1,0:T(1,128)S(1)}, s32[1,1,24,1]{2,3,1,0:T(1,128)}, u32[]{:S(2)}) copy-start(s32[1,1,24,1]{2,3,1,0:T(1,128)} %param.23) | copy-start | bytes 292
  135.8 1.6 copy-start.9
  138.4 15.1 %collective-permute-start.2 = (f32[2,128,768]{2,1,0:T(8,128)}, f32[2,128,768]{2,1,0:T(8,128)S(1)}, u32[]{:S(2)}, u32[]{:S(2)}) collective-permute-start(f32[2,128,768]{2,1,0:T(8,128)} %get-tuple-element.67), channel_id=1, source_target_pairs={{0,1},{1,2},{2,3},{3,4},{4,5},{5,6},{6,7},{8,9},{9,10},{10,11},{11... | collective-permute-start | bytes 2359304 | tf_op jit(solution)/shard_map/ppermute | solution.py:264
  144.3 13.3 %collective-permute-start.3 = (f32[2,128,768]{2,1,0:T(8,128)S(1)}, f32[2,128,768]{2,1,0:T(8,128)S(1)}, u32[]{:S(2)}, u32[]{:S(2)}) collective-permute-start(f32[2,128,768]{2,1,0:T(8,128)S(1)} %get-tuple-element.68), channel_id=1, source_target_pairs={{1,0},{2,1},{3,2},{4,3},{5,4},{6,5},{7,6},{9,8},{10,9},{11,10},{12... | collective-permute-start | bytes 2359304 | tf_op jit(solution)/shard_map/ppermute | solution.py:265
  159.8 2.7 %copy-start.3 = (bf16[2,2,256,256]{3,2,1,0:T(8,128)(2,1)S(1)}, bf16[2,2,256,256]{3,2,1,0:T(8,128)(2,1)}, u32[]{:S(2)}) copy-start(bf16[2,2,256,256]{3,2,1,0:T(8,128)(2,1)} %constant.122.clone.right_ref) | copy-start | bytes 1572868
  159.8 2.7 %copy-start.4 = (bf16[2,2,256,256]{3,2,1,0:T(8,128)(2,1)S(1)}, bf16[2,2,256,256]{3,2,1,0:T(8,128)(2,1)}, u32[]{:S(2)}) copy-start(bf16[2,2,256,256]{3,2,1,0:T(8,128)(2,1)} %constant.121.clone.left_ref) | copy-start | bytes 1572868
  162.5 17.6 %copy-start.1 = (f32[16,256,256]{2,1,0:T(8,128)S(1)}, f32[16,256,256]{2,1,0:T(8,128)}, u32[]{:S(2)}) copy-start(f32[16,256,256]{2,1,0:T(8,128)} %all_to_all.10.frame_ref) | copy-start | bytes 12582916
  180.1 15.4 %copy-start.6 = (bf16[256,256]{1,0:T(8,128)(2,1)S(1)}, bf16[256,256]{1,0:T(8,128)(2,1)}, u32[]{:S(2)}) copy-start(bf16[256,256]{1,0:T(8,128)(2,1)} %constant.124.clone.rest_0_) | copy-start | bytes 393220
  193.4 2.1 copy-start
  205.7 24.7 %collective-permute-start.4 = (f32[2,768,128]{2,1,0:T(8,128)S(1)}, f32[2,768,128]{2,1,0:T(8,128)S(1)}, u32[]{:S(2)}, u32[]{:S(2)}) collective-permute-start(f32[2,768,128]{2,1,0:T(8,128)S(1)} %get-tuple-element.64), channel_id=1, source_target_pairs={{0,8},{8,16},{16,24},{24,32},{32,40},{40,48},{48,56},{56,64},{64,7... | collective-permute-start | bytes 2359304 | tf_op jit(solution)/shard_map/ppermute | solution.py:274
  207.7 24.2 %collective-permute-start.5 = (f32[2,768,128]{2,1,0:T(8,128)S(1)}, f32[2,768,128]{2,1,0:T(8,128)S(1)}, u32[]{:S(2)}, u32[]{:S(2)}) collective-permute-start(f32[2,768,128]{2,1,0:T(8,128)S(1)} %get-tuple-element.63), channel_id=1, source_target_pairs={{8,0},{16,8},{24,16},{32,24},{40,32},{48,40},{56,48},{64,56},{72,6... | collective-permute-start | bytes 2359304 | tf_op jit(solution)/shard_map/ppermute | solution.py:274
  232.2 20.0 %collective-permute-start.6 = (f32[2,128,512]{2,1,0:T(8,128)S(1)}, f32[2,128,512]{2,1,0:T(8,128)S(1)}, u32[]{:S(2)}, u32[]{:S(2)}) collective-permute-start(f32[2,128,512]{2,1,0:T(8,128)S(1)} %get-tuple-element.66), channel_id=1, source_target_pairs={{0,1},{1,2},{2,3},{3,4},{4,5},{5,6},{6,7},{8,9},{9,10},{10,11},{11... | collective-permute-start | bytes 1572872 | tf_op jit(solution)/shard_map/ppermute | solution.py:274
  246.0 10.8 %copy-start.8 = (f32[2,512,512]{2,1,0:T(8,128)S(1)}, f32[2,512,512]{2,1,0:T(8,128)}, u32[]{:S(2)}) copy-start(f32[2,512,512]{2,1,0:T(8,128)} %param.19) | copy-start | bytes 6291460
  246.1 10.6 %collective-permute-start.7 = (f32[2,128,512]{2,1,0:T(8,128)S(1)}, f32[2,128,512]{2,1,0:T(8,128)S(1)}, u32[]{:S(2)}, u32[]{:S(2)}) collective-permute-start(f32[2,128,512]{2,1,0:T(8,128)S(1)} %get-tuple-element.65), channel_id=1, source_target_pairs={{1,0},{2,1},{3,2},{4,3},{5,4},{6,5},{7,6},{9,8},{10,9},{11,10},{12... | collective-permute-start | bytes 1572872 | tf_op jit(solution)/shard_map/ppermute | solution.py:274

commit v3 on v2

v3 whole, which is shorter than its diff:
```python
import functools

import jax
import jax.numpy as jnp
import ml_dtypes
import numpy as np
from jax import lax
from jax.experimental import pallas as pl
from jax.experimental.pallas import tpu as pltpu
from jax.sharding import PartitionSpec as P


PATCH = 256
HALF = 128
TASKS = 24
TILE = 512
BLOCKS = 3
EXT = 768


step_size = 0.1
ridge = 0.5

f32 = jnp.float32
bf16 = jnp.bfloat16


def tables():
    j = np.arange(HALF)
    even = np.exp(-2j * np.pi * (np.outer(j, 2 * j) % PATCH) / PATCH) / 16.0
    odd = np.exp(-2j * np.pi * (np.outer(j, 2 * j + 1) % PATCH) / PATCH) / 16.0

    def left(w):
        return np.block([[w.real, -w.imag], [w.imag, w.real]])

    def split(w):
        high = w.astype(ml_dtypes.bfloat16)
        low = (w - high.astype(np.float64)).astype(ml_dtypes.bfloat16)
        return high, low

    pairs = [split(left(w)) for w in (even, odd)]
    lefts = np.stack([np.stack(pair) for pair in pairs])
    return jnp.asarray(lefts), jnp.asarray(np.swapaxes(lefts, 2, 3).copy())


def shuffle():
    p = np.zeros((PATCH, PATCH), np.float32)
    j = np.arange(HALF)
    p[2 * j, j] = 1
    p[2 * j + 1, HALF + j] = 1
    return p.astype(ml_dtypes.bfloat16)


def two_terms(x):
    high = x.astype(bf16)
    low = (x - high.astype(f32)).astype(bf16)
    return high, low


def three_dot(x, p):
    high = x.astype(bf16)
    rest = x - high.astype(f32)
    mid = rest.astype(bf16)
    low = (rest - mid.astype(f32)).astype(bf16)
    out = jnp.dot(high, p, preferred_element_type=f32)
    out = out + jnp.dot(mid, p, preferred_element_type=f32)
    return out + jnp.dot(low, p, preferred_element_type=f32)


def spread(value, perm_ref, out_ref, c, b, even_ref, odd_ref):
    rows = value.shape[0]
    mixed = three_dot(value, perm_ref[...])
    even_ref[:rows] = mixed[:, :HALF]
    odd_ref[:rows] = mixed[:, HALF:]
    for q in range(2):
        out_ref[c, 0, b, q] = even_ref[pl.ds(q, rows // 2, stride=2), :]
        out_ref[c, 1, b, q] = odd_ref[pl.ds(q, rows // 2, stride=2), :]


def prep_kernel(*refs):
    perm_ref, probe_out, out_ref, even_ref, odd_ref = refs[6:11]
    probe_ref, tile_ref, left_ref, right_ref, up_ref, down_ref = refs[11:17]
    copies = [pltpu.make_async_copy(refs[i], refs[11 + i], refs[17].at[i]) for i in range(6)]
    for copy in copies:
        copy.start()
    for copy in copies:
        copy.wait()
    size = tile_ref.shape[2]
    for c in range(2):
        spread(probe_ref[c], perm_ref, probe_out, c, 0, even_ref, odd_ref)
        for b in range(BLOCKS):
            if b == 0:
                middle = jnp.concatenate([left_ref[c], tile_ref[c, :, :HALF]], axis=1)
            elif b == 1:
                middle = tile_ref[c, :, HALF : size - HALF]
            else:
                middle = jnp.concatenate([tile_ref[c, :, size - HALF :], right_ref[c]], axis=1)
            cols = slice(b * PATCH, (b + 1) * PATCH)
            value = jnp.concatenate([up_ref[c, :, cols], middle, down_ref[c, :, cols]], axis=0)
            spread(value, perm_ref, out_ref, c, b, even_ref, odd_ref)


def prep(probe, pieces):
    return pl.pallas_call(
        prep_kernel,
        out_shape=(
            jax.ShapeDtypeStruct((2, 2, 1, 2, HALF, HALF), f32),
            jax.ShapeDtypeStruct((2, 2, BLOCKS, 2, EXT // 2, HALF), f32),
        ),
        in_specs=[pl.BlockSpec(memory_space=pl.ANY)] * 6 + [pl.BlockSpec(memory_space=pltpu.VMEM)],
        out_specs=[pl.BlockSpec(memory_space=pltpu.VMEM)] * 2,
        scratch_shapes=[pltpu.VMEM((EXT, HALF), f32)] * 2
        + [pltpu.VMEM(x.shape, f32) for x in (probe, *pieces)]
        + [pltpu.SemaphoreType.DMA((6,))],
        compiler_params=pltpu.CompilerParams(vmem_limit_bytes=40 << 20),
        cost_estimate=pl.CostEstimate(flops=6 * EXT * EXT * PATCH * 2, bytes_accessed=16 * EXT * EXT, transcendentals=0),
    )(probe, *pieces, jnp.asarray(shuffle()))


def window(pos_ref, t):
    start_y = pos_ref[2 * t] + HALF
    start_x = pos_ref[2 * t + 1] + HALF
    block = jnp.where(start_x >= PATCH, 1, 0)
    offset = start_x - block * PATCH
    rows = [((start_y + q) & 1, (start_y + q) >> 1) for q in range(2)]
    return block, offset, rows


def rolled_probe(probe_ref, offset, p, q):
    source = (p + offset) & 1
    amount = ((offset + source - p) >> 1) & (HALF - 1)
    return [pltpu.roll(probe_ref[c, source, 0, q], amount, 1) for c in range(2)]


def lane_mask(offset, p):
    lane = lax.broadcasted_iota(jnp.int32, (HALF, HALF), 1)
    return lane >= ((offset + 1 - p) >> 1)


def put(high_ref, low_ref, where, value):
    high, low = two_terms(value)
    high_ref[where] = high
    low_ref[where] = low


def right_from(high_ref, low_ref, k, w_ref):
    high = high_ref[k]
    w = w_ref[k, 0]
    out = jnp.dot(
        jnp.concatenate([high, low_ref[k], high], axis=1),
        jnp.concatenate([w, w, w_ref[k, 1]], axis=0),
        preferred_element_type=f32,
    )
    return out


def left_from(w_ref, high_ref, low_ref, k):
    high = high_ref[k]
    w = w_ref[k, 0]
    return jnp.dot(
        jnp.concatenate([w, w, w_ref[k, 1]], axis=1),
        jnp.concatenate([high, low_ref[k], high], axis=0),
        preferred_element_type=f32,
    )


def forward_kernel(pos_ref, count_ref, obj_ref, probe_ref, left_ref, right_ref, out_ref, *scratch):
    step = pl.program_id(0)

    @pl.when(2 * step < count_ref[0])
    def _():
        for k in range(2):
            ah_ref, al_ref = scratch[4 * k : 4 * k + 2]
            block, offset, rows = window(pos_ref, 2 * step + k)
            for p in range(2):
                mask = lane_mask(offset, p)
                for q in range(2):
                    parity, first = rows[q]
                    o = [
                        jnp.where(
                            mask,
                            obj_ref[c, p, block, parity, pl.ds(first, HALF), :],
                            obj_ref[c, p, block + 1, parity, pl.ds(first, HALF), :],
                        )
                        for c in range(2)
                    ]
                    w = rolled_probe(probe_ref, offset, p, q)
                    r = slice(q * HALF, (q + 1) * HALF)
                    put(ah_ref, al_ref, (p, r, slice(0, HALF)), w[0] * o[0] - w[1] * o[1])
                    put(ah_ref, al_ref, (p, r, slice(HALF, PATCH)), w[0] * o[1] + w[1] * o[0])
        for k in range(2):
            ah_ref, al_ref, bh_ref, bl_ref = scratch[4 * k : 4 * k + 4]
            even = right_from(ah_ref, al_ref, 0, right_ref)
            odd = right_from(ah_ref, al_ref, 1, right_ref)
            for q in range(2):
                r = slice(q * HALF, (q + 1) * HALF)
                for c in range(2):
                    lanes = slice(c * HALF, (c + 1) * HALF)
                    put(bh_ref, bl_ref, (q, lanes, slice(0, HALF)), even[r, lanes] + odd[r, lanes])
                    put(bh_ref, bl_ref, (q, lanes, slice(HALF, PATCH)), even[r, lanes] - odd[r, lanes])
        for k in range(2):
            bh_ref, bl_ref = scratch[4 * k + 2 : 4 * k + 4]
            even = left_from(left_ref, bh_ref, bl_ref, 0)
            odd = left_from(left_ref, bh_ref, bl_ref, 1)
            out_ref[k, 0] = even + odd
            out_ref[k, 1] = even - odd


def forward(pos, count, obj, probe, lefts, rights):
    whole = pl.BlockSpec(memory_space=pltpu.VMEM)
    return pl.pallas_call(
        forward_kernel,
        out_shape=jax.ShapeDtypeStruct((TASKS, 2, PATCH, PATCH), f32),
        grid_spec=pltpu.PrefetchScalarGridSpec(
            num_scalar_prefetch=2,
            grid=(TASKS // 2,),
            in_specs=[whole] * 4,
            out_specs=pl.BlockSpec((2, 2, PATCH, PATCH), lambda t, pos, count: (t, 0, 0, 0)),
            scratch_shapes=[pltpu.VMEM((2, PATCH, PATCH), bf16)] * 8,
        ),
        compiler_params=pltpu.CompilerParams(vmem_limit_bytes=40 << 20),
        cost_estimate=pl.CostEstimate(flops=TASKS * 24 * PATCH**3, bytes_accessed=TASKS * 8 * PATCH**2, transcendentals=0),
    )(pos, count, obj, probe, lefts, rights)


def inverse_kernel(last, pos_ref, order_ref, slot_ref, count_ref, far_0, far_1, frame_0, frame_1, probe_ref, left_ref, right_ref, *rest):
    if last:
        perm_ref, before_ref = rest[:2]
        outs = rest[2:7]
        scratch = rest[7:15]
        acc_ref, even_ref, odd_ref, earlier_ref, sem = rest[15:]
        load = pltpu.make_async_copy(before_ref, earlier_ref, sem)
    else:
        acc_ref = rest[0]
        scratch = rest[1:]
    i = pl.program_id(0)

    @pl.when(i == 0)
    def _():
        if last:
            load.start()
        acc_ref[...] = jnp.zeros_like(acc_ref)

    @pl.when(2 * i < count_ref[0])
    def _():
        for k, far_ref, frame_ref in ((0, far_0, frame_0), (1, far_1, frame_1)):
            sh_ref, sl_ref = scratch[4 * k : 4 * k + 2]
            step = 32
            for at in range(0, HALF, step):
                parts = []
                for h in range(2):
                    re = far_ref[0, h, at : at + step, :]
                    im = far_ref[0, h, HALF + at : HALF + at + step, :]
                    weight = re * re + im * im - frame_ref[0, h * HALF + at : h * HALF + at + step, :]
                    parts.append((weight * re, weight * im))
                for c in range(2):
                    r = slice(c * HALF + at, c * HALF + at + step)
                    put(sh_ref, sl_ref, (0, r), parts[0][c] + parts[1][c])
                    put(sh_ref, sl_ref, (1, r), parts[0][c] - parts[1][c])
        for k in range(2):
            sh_ref, sl_ref, th_ref, tl_ref = scratch[4 * k : 4 * k + 4]
            for q in range(2):
                back = left_from(right_ref, sh_ref, sl_ref, q)
                r = slice(q * HALF, (q + 1) * HALF)
                for c in range(2):
                    lanes = slice(c * HALF, (c + 1) * HALF)
                    low, high = back[lanes, :HALF], back[lanes, HALF:]
                    put(th_ref, tl_ref, (0, r, lanes), low + high)
                    put(th_ref, tl_ref, (1, r, lanes), low - high)
        for k in range(2):
            th_ref, tl_ref = scratch[4 * k + 2 : 4 * k + 4]
            block, offset, rows = window(pos_ref, order_ref[2 * i + k])
            live = 2 * i + k < count_ref[0]
            for p in range(2):
                chi = right_from(th_ref, tl_ref, p, left_ref)
                mask = lane_mask(offset, p)
                for q in range(2):
                    parity, first = rows[q]
                    w = rolled_probe(probe_ref, offset, p, q)
                    r = slice(q * HALF, (q + 1) * HALF)
                    re, im = chi[r, :HALF], chi[r, HALF:]
                    g = [w[0] * re + w[1] * im, w[0] * im - w[1] * re]
                    for c in range(2):
                        here = acc_ref.at[c, p, block, parity, pl.ds(first, HALF), :]
                        there = acc_ref.at[c, p, block + 1, parity, pl.ds(first, HALF), :]
                        value = jnp.where(mask, here[...], there[...]) + g[c]
                        pltpu.store(here, value, mask=jnp.logical_and(mask, live))
                        pltpu.store(there, value, mask=jnp.logical_and(jnp.logical_not(mask), live))

    if last:

        @pl.when(i == pl.num_programs(0) - 1)
        def _():
            load.wait()
            for c in range(2):
                for b in range(BLOCKS):
                    for q in range(2):
                        even_ref[pl.ds(q, EXT // 2, stride=2), :] = acc_ref[c, 0, b, q] + earlier_ref[c, 0, b, q]
                        odd_ref[pl.ds(q, EXT // 2, stride=2), :] = acc_ref[c, 1, b, q] + earlier_ref[c, 1, b, q]
                    high, low = two_terms(jnp.concatenate([even_ref[...], odd_ref[...]], axis=1))
                    value = jnp.dot(high, perm_ref[...], preferred_element_type=f32)
                    value = value + jnp.dot(low, perm_ref[...], preferred_element_type=f32)
                    cols = slice(b * PATCH, (b + 1) * PATCH)
                    outs[3][c, :, cols] = value[:HALF]
                    outs[4][c, :, cols] = value[HALF + TILE :]
                    middle = value[HALF : HALF + TILE]
                    if b == 0:
                        outs[1][c] = middle[:, :HALF]
                        outs[0][c, :, :HALF] = middle[:, HALF:]
                    elif b == 1:
                        outs[0][c, :, HALF : HALF + PATCH] = middle
                    else:
                        outs[0][c, :, HALF + PATCH :] = middle[:, :HALF]
                        outs[2][c] = middle[:, HALF:]


def inverse(last, most, pos, order, slot, count, far, frames, probe, lefts, rights, before=None):
    whole = pl.BlockSpec(memory_space=pltpu.VMEM)
    parts = (2, 2, BLOCKS, 2, EXT // 2, HALF)
    more = (jnp.asarray(shuffle().T.copy()), before) if last else ()
    more_specs = [whole, pl.BlockSpec(memory_space=pl.ANY)] if last else []
    strips = [pltpu.VMEM(parts, f32)] + [pltpu.VMEM((EXT, HALF), f32)] * 2 + [pltpu.VMEM(parts, f32), pltpu.SemaphoreType.DMA]

    sizes = ((TILE, TILE), (TILE, HALF), (TILE, HALF), (HALF, EXT), (HALF, EXT))

    def far_spec(k):
        return pl.BlockSpec((1, 2, PATCH, PATCH), lambda i, pos, order, slot, count: (order[2 * i + k], 0, 0, 0))

    def frame_spec(k):
        return pl.BlockSpec((1, PATCH, PATCH), lambda i, pos, order, slot, count: (slot[2 * i + k], 0, 0))

    return pl.pallas_call(
        functools.partial(inverse_kernel, last),
        out_shape=[jax.ShapeDtypeStruct((2,) + size, f32) for size in sizes] if last else jax.ShapeDtypeStruct(parts, f32),
        grid_spec=pltpu.PrefetchScalarGridSpec(
            num_scalar_prefetch=4,
            grid=(most // 2,),
            in_specs=[far_spec(0), far_spec(1), frame_spec(0), frame_spec(1)] + [whole] * 3 + more_specs,
            out_specs=[whole] * 5 if last else whole,
            scratch_shapes=[pltpu.VMEM((2, PATCH, PATCH), bf16)] * 8 + (strips if last else []),
        ),
        compiler_params=pltpu.CompilerParams(vmem_limit_bytes=40 << 20),
        cost_estimate=pl.CostEstimate(flops=most * 24 * PATCH**3, bytes_accessed=most * 12 * PATCH**2, transcendentals=0),
    )(pos, order, slot, count, far, far, frames, frames, probe, lefts, rights, *more)


def strips_kernel(object_ref, first_ref, last_ref, sem):
    size = object_ref.shape[2]
    copies = [
        pltpu.make_async_copy(object_ref.at[:, :, pl.ds(0, HALF)], first_ref, sem.at[0]),
        pltpu.make_async_copy(object_ref.at[:, :, pl.ds(size - HALF, HALF)], last_ref, sem.at[1]),
    ]
    for copy in copies:
        copy.start()
    for copy in copies:
        copy.wait()


def strips(block):
    strip = jax.ShapeDtypeStruct((2, block.shape[1], HALF), f32)
    return pl.pallas_call(
        strips_kernel,
        out_shape=(strip, strip),
        in_specs=[pl.BlockSpec(memory_space=pl.ANY)],
        out_specs=[pl.BlockSpec(memory_space=pltpu.VMEM)] * 2,
        scratch_shapes=[pltpu.SemaphoreType.DMA((2,))],
        compiler_params=pltpu.CompilerParams(vmem_limit_bytes=62 << 20),
        cost_estimate=pl.CostEstimate(flops=0, bytes_accessed=2 << 20, transcendentals=0),
    )(block)


def pick_kernel(slot, frames_ref, out_ref, buffer_ref, sem):
    count = sem.shape[1]
    size = out_ref.shape[0] // count
    pieces = [pl.ds(i * size, size) for i in range(count)]
    loads = [pltpu.make_async_copy(frames_ref.at[p, slot], buffer_ref.at[p], sem.at[0, i]) for i, p in enumerate(pieces)]
    stores = [pltpu.make_async_copy(buffer_ref.at[p], out_ref.at[p], sem.at[1, i]) for i, p in enumerate(pieces)]
    for load in loads:
        load.start()
    for load, store in zip(loads, stores):
        load.wait()
        store.start()
    for store in stores:
        store.wait()


def pick(kept, slot):
    shape = (kept.shape[0], PATCH, PATCH)
    return pl.pallas_call(
        functools.partial(pick_kernel, slot),
        out_shape=jax.ShapeDtypeStruct(shape, f32),
        in_specs=[pl.BlockSpec(memory_space=pl.ANY)],
        out_specs=pl.BlockSpec(memory_space=pl.ANY),
        scratch_shapes=[pltpu.VMEM(shape, f32), pltpu.SemaphoreType.DMA((2, 4))],
        compiler_params=pltpu.CompilerParams(vmem_limit_bytes=58 << 20),
        cost_estimate=pl.CostEstimate(flops=0, bytes_accessed=8 << 20, transcendentals=0),
    )(kept)


def from_tile(sent, dy, dx):
    high, wide = lax.axis_size("gy"), lax.axis_size("gx")
    if dy == 0:
        return lax.ppermute(sent, "gx", [(i + dx, i) for i in range(wide) if 0 <= i + dx < wide])
    return lax.ppermute(sent, "gy", [(i + dy, i) for i in range(high) if 0 <= i + dy < high])


def final_kernel(object_ref, total_ref, left_ref, right_ref, up_ref, down_ref, left_ends, right_ends, out_ref):
    out_ref[...] = (1.0 - step_size * ridge) * object_ref[...] - step_size * total_ref[...]
    top, bottom = slice(0, HALF), slice(TILE - HALF, TILE)
    for rows, ref, at in ((top, up_ref, 0), (bottom, down_ref, HALF)):
        out_ref[:, rows, :] = out_ref[:, rows, :] - step_size * ref[:, :, HALF : HALF + TILE]
        for lanes, ends in ((top, left_ends), (bottom, right_ends)):
            out_ref[:, rows, lanes] = out_ref[:, rows, lanes] - step_size * ends[:, at : at + HALF]
    out_ref[:, :, top] = out_ref[:, :, top] - step_size * left_ref[...]
    out_ref[:, :, bottom] = out_ref[:, :, bottom] - step_size * right_ref[...]


def final(block, *parts):
    return pl.pallas_call(
        final_kernel,
        out_shape=jax.ShapeDtypeStruct(block.shape, f32),
        in_specs=[pl.BlockSpec(memory_space=pltpu.VMEM)] * 8,
        out_specs=pl.BlockSpec(memory_space=pltpu.VMEM),
        compiler_params=pltpu.CompilerParams(vmem_limit_bytes=16 << 20),
        cost_estimate=pl.CostEstimate(flops=4 * block.size, bytes_accessed=16 * block.size, transcendentals=0),
    )(block, *parts)


def ordered(chosen, helper_cols, most):
    task_ids = jnp.arange(TASKS, dtype=jnp.int32)
    place = jnp.sum(jnp.logical_and(chosen[None, :], task_ids[None, :] < task_ids[:, None]), axis=1)
    spot = jnp.logical_and(chosen[None, :], place[None, :] == jnp.arange(most)[:, None])
    order = jnp.sum(jnp.where(spot, task_ids[None, :], 0), axis=1).astype(jnp.int32)
    slot = jnp.sum(jnp.where(spot, helper_cols[None, :], 0), axis=1).astype(jnp.int32)
    return order, slot, jnp.sum(chosen).astype(jnp.int32).reshape(1)


def local(pieces, probe, arrived_0, arrived_1, offsets, helper_cols, count):
    task_ids = jnp.arange(TASKS, dtype=jnp.int32)
    same = helper_cols[:, None] == helper_cols[None, :]
    second = jnp.any(jnp.logical_and(same, task_ids[None, :] < task_ids[:, None]), axis=1)
    valid = task_ids < count[0]
    order_0 = ordered(jnp.logical_and(valid, jnp.logical_not(second)), helper_cols, 16)
    order_1 = ordered(jnp.logical_and(valid, second), helper_cols, TASKS // 2)
    lefts, rights = tables()
    pro, obj = prep(probe, pieces)
    far = forward(offsets, count, obj, pro, lefts, rights)
    part = inverse(False, 16, offsets, *order_0, far, arrived_0, pro, lefts, rights)
    return inverse(True, TASKS // 2, offsets, *order_1, far, arrived_1, pro, lefts, rights, part)


def per_device(object_field, probe, frames, positions, helpers, task_counts):
    first, last = strips(object_field)
    kept = frames[0, 0]
    left, right = from_tile(last, 0, -1), from_tile(first, 0, 1)
    arrived_0 = lax.all_to_all(pick(kept, 0), "gx", split_axis=0, concat_axis=0, tiled=True)
    again, _ = lax.optimization_barrier((kept, arrived_0))
    arrived_1 = lax.all_to_all(pick(again, 1), "gx", split_axis=0, concat_axis=0, tiled=True)
    above = jnp.concatenate([left[:, -HALF:], object_field[:, -HALF:], right[:, -HALF:]], axis=2)
    below = jnp.concatenate([left[:, :HALF], object_field[:, :HALF], right[:, :HALF]], axis=2)
    up, down = from_tile(above, -1, 0), from_tile(below, 1, 0)
    parts = local(
        [object_field, left, right, up, down],
        probe,
        arrived_0,
        arrived_1,
        positions[0, 0].reshape(-1),
        helpers[0, 0, :, 0],
        task_counts[0],
    )
    middle, to_left, to_right, to_up, to_down = parts
    up, down = from_tile(to_down, -1, 0), from_tile(to_up, 1, 0)
    left, right = from_tile(to_right, 0, -1), from_tile(to_left, 0, 1)
    first_ends = jnp.concatenate([up[:, :, :HALF], down[:, :, :HALF]], axis=1)
    last_ends = jnp.concatenate([up[:, :, -HALF:], down[:, :, -HALF:]], axis=1)
    left_ends, right_ends = from_tile(last_ends, 0, -1), from_tile(first_ends, 0, 1)
    return final(object_field, middle, left, right, up, down, left_ends, right_ends)


def solution(mesh):
    in_specs = (
        P(None, "gy", "gx"),
        P(),
        P("gy", "gx", None, None, None, None),
        P("gy", "gx", None, None),
        P("gy", "gx", None, None),
        P("gy", "gx"),
    )
    out_specs = P(None, "gy", "gx")
    return jax.shard_map(per_device, mesh=mesh, in_specs=in_specs, out_specs=out_specs, check_vma=False)
```

time: 260 us -> 242 us (0.931)
  the two profiles are of different devices: /device:TPU:65 before, /device:TPU:91 now
where the time goes in v3:
time: 242 us; the launch traced here: 240 us
  waiting for transfers between devices  85.2 us (35%)
  Pallas kernels  53.4 us (22%)
  blocking collectives  53.2 us (22%)
  starting transfers between devices  36 us (15%)
  local copies, waits for them, and re-layouts  8.58 us (4%)
  other arithmetic  3.08 us (1%)
    ppermute x6, waiting for transfers between devices, from_tile(): lax.ppermute(sent, 'gx', [(i + dx, i) for i in range(wide) if 0 <= i + dx...  68.8 us
    all_to_all x1, blocking collectives, per_device(): lax.all_to_all(pick(kept, 0), 'gx', split_axis=0, concat_axis=0, tiled=True)  53.2 us
    pallas_call x2, Pallas kernels, inverse(): pl.pallas_call(functools.partial(inverse_kernel, last), out_shape=[jax.Sh...  22 us
    ppermute x4, waiting for transfers between devices, from_tile(): lax.ppermute(sent, 'gy', [(i + dy, i) for i in range(high) if 0 <= i + dy...  16.4 us
    ppermute x6, starting transfers between devices, from_tile(): lax.ppermute(sent, 'gx', [(i + dx, i) for i in range(wide) if 0 <= i + dx...  16 us
    pallas_call x1, Pallas kernels, forward(): pl.pallas_call(forward_kernel, out_shape=jax.ShapeDtypeStruct((TASKS, 2,...  15.6 us
    ppermute x4, starting transfers between devices, from_tile(): lax.ppermute(sent, 'gy', [(i + dy, i) for i in range(high) if 0 <= i + dy...  12.2 us
    all_to_all x1, starting transfers between devices, per_device(): lax.all_to_all(pick(again, 1), 'gx', split_axis=0, concat_axis=0, tiled=T...  7.83 us
  transfers between devices with their start and end apart: 11, of which 8 were waited for; matrix products, arithmetic and copies ran while one was open for 2% of the time, Pallas kernels for 14%

profile of v3, /device:TPU:91, one launch (start us, length us, event | category | flops | bytes accessed | tf_op | source)
XLA Modules:
  0.0 240.4 jit_solution(8943566696737773469)
XLA Ops:
  0.0 3.3 %shard_map.103 = f32[16,256,256]{2,1,0:T(8,128)} custom-call(f32[16,2,256,256]{3,2,1,0:T(8,128)} %bitcast.10), custom_call_target="tpu_custom_call" | custom-call | bytes 8388608 | tf_op jit(solution)/shard_map/pallas_call | solution.py:389
  3.3 53.2 %all_to_all.10.frame_0.frame_1 = f32[16,256,256]{2,1,0:T(8,128)} all-to-all(f32[16,256,256]{2,1,0:T(8,128)} %shard_map.103), channel_id=1, replica_groups=mesh['gx'=16,'gy'=8] {'gx'}, dimensions={0} | all-to-all | bytes 8388608 | tf_op jit(solution)/shard_map/all_to_all | solution.py:456
  56.5 3.3 %shard_map.104 = f32[16,256,256]{2,1,0:T(8,128)} custom-call(f32[16,2,256,256]{3,2,1,0:T(8,128)} %bitcast.11), custom_call_target="tpu_custom_call" | custom-call | bytes 8388608 | tf_op jit(solution)/shard_map/pallas_call | solution.py:389
  59.8 7.8 %all-to-all-start.1 = ((f32[16,256,256]{2,1,0:T(8,128)}), f32[16,256,256]{2,1,0:T(8,128)}, u32[]{:S(2)}, u32[]{:S(2)}) async-start(f32[16,256,256]{2,1,0:T(8,128)} %shard_map.104), calls=%async_computation.1 | async-start | bytes 8388608 | tf_op jit(solution)/shard_map/all_to_all | solution.py:458
  67.7 2.2 shard_map.100
  69.9 2.9 %collective-permute-start = (f32[2,512,128]{2,1,0:T(8,128)}, f32[2,512,128]{2,1,0:T(8,128)S(1)}, u32[]{:S(2)}, u32[]{:S(2)}) collective-permute-start(f32[2,512,128]{2,1,0:T(8,128)} %get-tuple-element.15), channel_id=1, source_target_pairs={{0,8},{8,16},{16,24},{24,32},{32,40},{40,48},{48,56},{56,64},{64,7... | collective-permute-start | bytes 1572872 | tf_op jit(solution)/shard_map/ppermute | solution.py:403
  72.9 2.5 %collective-permute-start.1 = (f32[2,512,128]{2,1,0:T(8,128)}, f32[2,512,128]{2,1,0:T(8,128)S(1)}, u32[]{:S(2)}, u32[]{:S(2)}) collective-permute-start(f32[2,512,128]{2,1,0:T(8,128)} %get-tuple-element.16), channel_id=1, source_target_pairs={{8,0},{16,8},{24,16},{32,24},{40,32},{48,40},{56,48},{64,56},{72,6... | collective-permute-start | bytes 1572872 | tf_op jit(solution)/shard_map/ppermute | solution.py:403
  76.7 60.9 %collective-permute-done.refs_2_ = f32[2,512,128]{2,1,0:T(8,128)S(1)} collective-permute-done((f32[2,512,128]{2,1,0:T(8,128)}, f32[2,512,128]{2,1,0:T(8,128)S(1)}, u32[]{:S(2)}, u32[]{:S(2)}) %collective-permute-start) | collective-permute-done | bytes 524320 | tf_op jit(solution)/shard_map/ppermute | solution.py:403
  139.3 6.0 %collective-permute-start.2 = (f32[2,128,768]{2,1,0:T(8,128)}, f32[2,128,768]{2,1,0:T(8,128)}, u32[]{:S(2)}, u32[]{:S(2)}) collective-permute-start(f32[2,128,768]{2,1,0:T(8,128)} %pad_maximum_fusion), channel_id=1, source_target_pairs={{0,1},{1,2},{2,3},{3,4},{4,5},{5,6},{6,7},{8,9},{9,10},{10,11},{11... | collective-permute-start | bytes 2359304 | tf_op jit(solution)/shard_map/ppermute | solution.py:404
  150.2 4.3 %collective-permute-done.2.refs_4_ = f32[2,128,768]{2,1,0:T(8,128)} collective-permute-done((f32[2,128,768]{2,1,0:T(8,128)}, f32[2,128,768]{2,1,0:T(8,128)}, u32[]{:S(2)}, u32[]{:S(2)}) %collective-permute-start.2) | collective-permute-done | bytes 786464 | tf_op jit(solution)/shard_map/ppermute | solution.py:404
  154.5 5.3 %collective-permute-done.3.refs_5_ = f32[2,128,768]{2,1,0:T(8,128)} collective-permute-done((f32[2,128,768]{2,1,0:T(8,128)}, f32[2,128,768]{2,1,0:T(8,128)}, u32[]{:S(2)}, u32[]{:S(2)}) %collective-permute-start.3) | collective-permute-done | bytes 786464 | tf_op jit(solution)/shard_map/ppermute | solution.py:404
  163.0 4.6 %shard_map.101 = (f32[2,2,1,2,128,128]{5,4,3,2,1,0:T(8,128)S(1)}, f32[2,2,3,2,384,128]{5,4,3,2,1,0:T(8,128)S(1)}) custom-call(f32[2,256,256]{2,1,0:T(8,128)S(1)} %copy-done.12, f32[2,512,512]{2,1,0:T(8,128)S(1)} %copy-done.2, f32[2,512,128]{2,1,0:T(8,128)S(1)} %copy-done.9, f32[2,512,128]{2,1,0:T(8,128)S(1)} %copy-done.11, ...), custom_call_target="tpu_custom_call" | custom-call | flops 1811939328 | bytes 9437184 | tf_op jit(solution)/shard_map/pallas_call | solution.py:104
  167.6 15.6 %shard_map.102.far_0.far_1 = f32[24,2,256,256]{3,2,1,0:T(8,128)} custom-call(s32[48]{0:T(128)S(1)} %reshape_squeeze.3.pos_ref, s32[1]{0:T(128)} %bitcast.9.count_ref, f32[2,2,3,2,384,128]{5,4,3,2,1,0:T(8,128)S(1)} %get-tuple-element.17.obj_ref, f32[2,2,1,2,128,128]{5,4,3,2,1,0:T(8,128)S(1)} %get-tuple-element.18.probe_ref, ...), custom_call_target="tpu_custom_call" | custom-call | flops 9663676416 | bytes 12582912 | tf_op jit(solution)/shard_map/pallas_call | solution.py:211
  183.2 11.7 %shard_map.105.rest_1_ = f32[2,2,3,2,384,128]{5,4,3,2,1,0:T(8,128)S(1)} custom-call(s32[48]{0:T(128)S(1)} %reshape_squeeze.3.pos_ref, s32[16]{0:T(128)S(1)} %get-tuple-element.26.order_ref, s32[16]{0:T(128)S(1)} %get-tuple-element.25.slot_ref, s32[1]{0:T(128)} %bitcast.5.count_ref, f32[24,2,256,256]{3,2,1,0:T(8,128)} %shard_map.102.far_0.far_1, ...), custom_call_target="tpu_custom_call" | custom-call | flops 6442450944 | bytes 12582912 | tf_op jit(solution)/shard_map/pallas_call | solution.py:332
  194.9 2.1 copy-done.1
  198.0 10.3 %shard_map.106 = (f32[2,512,512]{2,1,0:T(8,128)S(1)}, f32[2,512,128]{2,1,0:T(8,128)S(1)}, f32[2,512,128]{2,1,0:T(8,128)S(1)}, f32[2,128,768]{2,1,0:T(8,128)S(1)}, f32[2,128,768]{2,1,0:T(8,128)S(1)}) custom-call(s32[48]{0:T(128)S(1)} %reshape_squeeze.3.pos_ref, s32[12]{0:T(128)S(1)} %get-tuple-element.28.order_ref, s32[12]{0:T(128)S(1)} %get-tuple-element.27.slot_ref, ...), custom_call_target="tpu_custom_call" | custom-call | flops 4831838208 | bytes 9437184 | tf_op jit(solution)/shard_map/pallas_call | solution.py:332
  210.3 2.4 %collective-permute-start.7 = (f32[2,128,768]{2,1,0:T(8,128)S(1)}, f32[2,128,768]{2,1,0:T(8,128)S(1)}, u32[]{:S(2)}, u32[]{:S(2)}) collective-permute-start(f32[2,128,768]{2,1,0:T(8,128)S(1)} %get-tuple-element.24), channel_id=1, source_target_pairs={{1,0},{2,1},{3,2},{4,3},{5,4},{6,5},{7,6},{9,8},{10,9},{11,10},{12... | collective-permute-start | bytes 2359304 | tf_op jit(solution)/shard_map/ppermute | solution.py:404
  212.7 1.9 collective-permute-start.4
  214.6 3.4 %collective-permute-start.5 = (f32[2,512,128]{2,1,0:T(8,128)S(1)}, f32[2,512,128]{2,1,0:T(8,128)S(1)}, u32[]{:S(2)}, u32[]{:S(2)}) collective-permute-start(f32[2,512,128]{2,1,0:T(8,128)S(1)} %get-tuple-element.22), channel_id=1, source_target_pairs={{8,0},{16,8},{24,16},{32,24},{40,32},{48,40},{56,48},{64,56},{72,6... | collective-permute-start | bytes 1572872 | tf_op jit(solution)/shard_map/ppermute | solution.py:403
  219.2 5.5 %collective-permute-done.7.down_ref = f32[2,128,768]{2,1,0:T(8,128)S(1)} collective-permute-done((f32[2,128,768]{2,1,0:T(8,128)S(1)}, f32[2,128,768]{2,1,0:T(8,128)S(1)}, u32[]{:S(2)}, u32[]{:S(2)}) %collective-permute-start.7) | collective-permute-done | bytes 786464 | tf_op jit(solution)/shard_map/ppermute | solution.py:404
  226.8 3.4 %collective-permute-start.9 = (f32[2,256,128]{2,1,0:T(8,128)S(1)}, f32[2,256,128]{2,1,0:T(8,128)S(1)}, u32[]{:S(2)}, u32[]{:S(2)}) collective-permute-start(f32[2,256,128]{2,1,0:T(8,128)S(1)} %pad_maximum_fusion.3), channel_id=1, source_target_pairs={{8,0},{16,8},{24,16},{32,24},{40,32},{48,40},{56,48},{64,56},{72,6... | collective-permute-start | bytes 786440 | tf_op jit(solution)/shard_map/ppermute | solution.py:403
  230.7 3.7 %collective-permute-done.8.left_ends = f32[2,256,128]{2,1,0:T(8,128)S(1)} collective-permute-done((f32[2,256,128]{2,1,0:T(8,128)S(1)}, f32[2,256,128]{2,1,0:T(8,128)S(1)}, u32[]{:S(2)}, u32[]{:S(2)}) %collective-permute-start.8) | collective-permute-done | bytes 262176 | tf_op jit(solution)/shard_map/ppermute | solution.py:403
  234.4 3.8 %collective-permute-done.9.right_ends = f32[2,256,128]{2,1,0:T(8,128)S(1)} collective-permute-done((f32[2,256,128]{2,1,0:T(8,128)S(1)}, f32[2,256,128]{2,1,0:T(8,128)S(1)}, u32[]{:S(2)}, u32[]{:S(2)}) %collective-permute-start.9) | collective-permute-done | bytes 262176 | tf_op jit(solution)/shard_map/ppermute | solution.py:403
  238.1 2.3 shard_map.107
  (55 shorter events, 17.1 us)
Async XLA Ops:
  59.8 137.2 %all-to-all-start.1 = ((f32[16,256,256]{2,1,0:T(8,128)}), f32[16,256,256]{2,1,0:T(8,128)}, u32[]{:S(2)}, u32[]{:S(2)}) async-start(f32[16,256,256]{2,1,0:T(8,128)} %shard_map.104), calls=%async_computation.1 | async-start | bytes 8388608 | tf_op jit(solution)/shard_map/all_to_all | solution.py:458
  67.6 81.2 %copy-start.15 = (s32[1,1,24,2]{2,3,1,0:T(2,128)S(1)}, s32[1,1,24,2]{2,3,1,0:T(2,128)}, u32[]{:S(2)}) copy-start(s32[1,1,24,2]{2,3,1,0:T(2,128)} %param.13) | copy-start | bytes 580
  67.7 81.3 %copy-start.14 = (s32[1,1,24,1]{2,3,1,0:T(1,128)S(1)}, s32[1,1,24,1]{2,3,1,0:T(1,128)}, u32[]{:S(2)}) copy-start(s32[1,1,24,1]{2,3,1,0:T(1,128)} %param.14) | copy-start | bytes 292
  67.7 92.2 %copy-start.13 = (bf16[256,256]{1,0:T(8,128)(2,1)S(1)}, bf16[256,256]{1,0:T(8,128)(2,1)}, u32[]{:S(2)}) copy-start(bf16[256,256]{1,0:T(8,128)(2,1)} %constant.14.clone.refs_6_) | copy-start | bytes 393220
  69.9 89.9 %copy-start.2 = (f32[2,512,512]{2,1,0:T(8,128)S(1)}, f32[2,512,512]{2,1,0:T(8,128)}, u32[]{:S(2)}) copy-start(f32[2,512,512]{2,1,0:T(8,128)} %object_ref.3) | copy-start | bytes 6291460
  69.9 67.6 %collective-permute-start = (f32[2,512,128]{2,1,0:T(8,128)}, f32[2,512,128]{2,1,0:T(8,128)S(1)}, u32[]{:S(2)}, u32[]{:S(2)}) collective-permute-start(f32[2,512,128]{2,1,0:T(8,128)} %get-tuple-element.15), channel_id=1, source_target_pairs={{0,8},{8,16},{16,24},{24,32},{32,40},{40,48},{48,56},{56,64},{64,7... | collective-permute-start | bytes 1572872 | tf_op jit(solution)/shard_map/ppermute | solution.py:403
  72.9 64.7 %collective-permute-start.1 = (f32[2,512,128]{2,1,0:T(8,128)}, f32[2,512,128]{2,1,0:T(8,128)S(1)}, u32[]{:S(2)}, u32[]{:S(2)}) collective-permute-start(f32[2,512,128]{2,1,0:T(8,128)} %get-tuple-element.16), channel_id=1, source_target_pairs={{8,0},{16,8},{24,16},{32,24},{40,32},{48,40},{56,48},{64,56},{72,6... | collective-permute-start | bytes 1572872 | tf_op jit(solution)/shard_map/ppermute | solution.py:403
  137.6 1.7 copy-start.10
  139.3 28.3 %copy-start.3 = (bf16[2,2,256,256]{3,2,1,0:T(8,128)(2,1)S(1)}, bf16[2,2,256,256]{3,2,1,0:T(8,128)(2,1)}, u32[]{:S(2)}) copy-start(bf16[2,2,256,256]{3,2,1,0:T(8,128)(2,1)} %constant.13.clone.right_ref) | copy-start | bytes 1572868
  139.3 28.3 %copy-start.4 = (bf16[2,2,256,256]{3,2,1,0:T(8,128)(2,1)S(1)}, bf16[2,2,256,256]{3,2,1,0:T(8,128)(2,1)}, u32[]{:S(2)}) copy-start(bf16[2,2,256,256]{3,2,1,0:T(8,128)(2,1)} %constant.12.clone.left_ref) | copy-start | bytes 1572868
  139.3 15.2 %collective-permute-start.2 = (f32[2,128,768]{2,1,0:T(8,128)}, f32[2,128,768]{2,1,0:T(8,128)}, u32[]{:S(2)}, u32[]{:S(2)}) collective-permute-start(f32[2,128,768]{2,1,0:T(8,128)} %pad_maximum_fusion), channel_id=1, source_target_pairs={{0,1},{1,2},{2,3},{3,4},{4,5},{5,6},{6,7},{8,9},{9,10},{10,11},{11... | collective-permute-start | bytes 2359304 | tf_op jit(solution)/shard_map/ppermute | solution.py:404
  146.2 13.6 %collective-permute-start.3 = (f32[2,128,768]{2,1,0:T(8,128)}, f32[2,128,768]{2,1,0:T(8,128)}, u32[]{:S(2)}, u32[]{:S(2)}) collective-permute-start(f32[2,128,768]{2,1,0:T(8,128)} %pad_maximum_fusion.1), channel_id=1, source_target_pairs={{1,0},{2,1},{3,2},{4,3},{5,4},{6,5},{7,6},{9,8},{10,9},{11,10},{12... | collective-permute-start | bytes 2359304 | tf_op jit(solution)/shard_map/ppermute | solution.py:404
  159.9 1.0 copy-start.9
  167.6 15.7 %copy-start.5 = (f32[2,2,1,2,128,128]{5,4,3,2,1,0:T(8,128)}, f32[2,2,1,2,128,128]{5,4,3,2,1,0:T(8,128)S(1)}, u32[]{:S(2)}) copy-start(f32[2,2,1,2,128,128]{5,4,3,2,1,0:T(8,128)S(1)} %get-tuple-element.18.probe_ref) | copy-start | bytes 1572868
  167.6 15.7 %copy-start = (f32[16,256,256]{2,1,0:T(8,128)S(1)}, f32[16,256,256]{2,1,0:T(8,128)}, u32[]{:S(2)}) copy-start(f32[16,256,256]{2,1,0:T(8,128)} %all_to_all.10.frame_0.frame_1) | copy-start | bytes 12582916
  183.2 13.8 %copy-start.7 = (bf16[256,256]{1,0:T(8,128)(2,1)S(1)}, bf16[256,256]{1,0:T(8,128)(2,1)}, u32[]{:S(2)}) copy-start(bf16[256,256]{1,0:T(8,128)(2,1)} %constant.15.clone.rest_0_) | copy-start | bytes 393220
  194.9 2.1 copy-start.1
  197.0 1.0 copy-start.6
  208.4 10.8 %collective-permute-start.6 = (f32[2,128,768]{2,1,0:T(8,128)S(1)}, f32[2,128,768]{2,1,0:T(8,128)S(1)}, u32[]{:S(2)}, u32[]{:S(2)}) collective-permute-start(f32[2,128,768]{2,1,0:T(8,128)S(1)} %get-tuple-element.23), channel_id=1, source_target_pairs={{0,1},{1,2},{2,3},{3,4},{4,5},{5,6},{6,7},{8,9},{9,10},{10,11},{11... | collective-permute-start | bytes 2359304 | tf_op jit(solution)/shard_map/ppermute | solution.py:404
  210.3 14.5 %collective-permute-start.7 = (f32[2,128,768]{2,1,0:T(8,128)S(1)}, f32[2,128,768]{2,1,0:T(8,128)S(1)}, u32[]{:S(2)}, u32[]{:S(2)}) collective-permute-start(f32[2,128,768]{2,1,0:T(8,128)S(1)} %get-tuple-element.24), channel_id=1, source_target_pairs={{1,0},{2,1},{3,2},{4,3},{5,4},{6,5},{7,6},{9,8},{10,9},{11,10},{12... | collective-permute-start | bytes 2359304 | tf_op jit(solution)/shard_map/ppermute | solution.py:404
  212.7 17.4 %collective-permute-start.4 = (f32[2,512,128]{2,1,0:T(8,128)S(1)}, f32[2,512,128]{2,1,0:T(8,128)S(1)}, u32[]{:S(2)}, u32[]{:S(2)}) collective-permute-start(f32[2,512,128]{2,1,0:T(8,128)S(1)} %get-tuple-element.21), channel_id=1, source_target_pairs={{0,8},{8,16},{16,24},{24,32},{32,40},{40,48},{48,56},{56,64},{64,7... | collective-permute-start | bytes 1572872 | tf_op jit(solution)/shard_map/ppermute | solution.py:403
  214.6 16.1 %collective-permute-start.5 = (f32[2,512,128]{2,1,0:T(8,128)S(1)}, f32[2,512,128]{2,1,0:T(8,128)S(1)}, u32[]{:S(2)}, u32[]{:S(2)}) collective-permute-start(f32[2,512,128]{2,1,0:T(8,128)S(1)} %get-tuple-element.22), channel_id=1, source_target_pairs={{8,0},{16,8},{24,16},{32,24},{40,32},{48,40},{56,48},{64,56},{72,6... | collective-permute-start | bytes 1572872 | tf_op jit(solution)/shard_map/ppermute | solution.py:403
  224.8 9.5 %collective-permute-start.8 = (f32[2,256,128]{2,1,0:T(8,128)S(1)}, f32[2,256,128]{2,1,0:T(8,128)S(1)}, u32[]{:S(2)}, u32[]{:S(2)}) collective-permute-start(f32[2,256,128]{2,1,0:T(8,128)S(1)} %pad_maximum_fusion.2), channel_id=1, source_target_pairs={{0,8},{8,16},{16,24},{24,32},{32,40},{40,48},{48,56},{56,64},{64,7... | collective-permute-start | bytes 786440 | tf_op jit(solution)/shard_map/ppermute | solution.py:403
  226.8 11.3 %collective-permute-start.9 = (f32[2,256,128]{2,1,0:T(8,128)S(1)}, f32[2,256,128]{2,1,0:T(8,128)S(1)}, u32[]{:S(2)}, u32[]{:S(2)}) collective-permute-start(f32[2,256,128]{2,1,0:T(8,128)S(1)} %pad_maximum_fusion.3), channel_id=1, source_target_pairs={{8,0},{16,8},{24,16},{32,24},{40,32},{48,40},{56,48},{64,56},{72,6... | collective-permute-start | bytes 786440 | tf_op jit(solution)/shard_map/ppermute | solution.py:403
  (3 other events, 2.9 us)

commit v4 on v3

--- a/solution.py
+++ b/solution.py
@@ -77,44 +77,54 @@
         out_ref[c, 1, b, q] = odd_ref[pl.ds(q, rows // 2, stride=2), :]
 
 
-def prep_kernel(*refs):
-    perm_ref, probe_out, out_ref, even_ref, odd_ref = refs[6:11]
-    probe_ref, tile_ref, left_ref, right_ref, up_ref, down_ref = refs[11:17]
-    copies = [pltpu.make_async_copy(refs[i], refs[11 + i], refs[17].at[i]) for i in range(6)]
-    for copy in copies:
-        copy.start()
-    for copy in copies:
-        copy.wait()
+def middle_kernel(probe_ref, tile_ref, left_ref, right_ref, perm_ref, probe_out, out_ref, even_ref, odd_ref):
     size = tile_ref.shape[2]
     for c in range(2):
         spread(probe_ref[c], perm_ref, probe_out, c, 0, even_ref, odd_ref)
         for b in range(BLOCKS):
             if b == 0:
-                middle = jnp.concatenate([left_ref[c], tile_ref[c, :, :HALF]], axis=1)
+                value = jnp.concatenate([left_ref[c], tile_ref[c, :, :HALF]], axis=1)
             elif b == 1:
-                middle = tile_ref[c, :, HALF : size - HALF]
+                value = tile_ref[c, :, HALF : size - HALF]
             else:
-                middle = jnp.concatenate([tile_ref[c, :, size - HALF :], right_ref[c]], axis=1)
-            cols = slice(b * PATCH, (b + 1) * PATCH)
-            value = jnp.concatenate([up_ref[c, :, cols], middle, down_ref[c, :, cols]], axis=0)
+                value = jnp.concatenate([tile_ref[c, :, size - HALF :], right_ref[c]], axis=1)
             spread(value, perm_ref, out_ref, c, b, even_ref, odd_ref)
 
 
-def prep(probe, pieces):
-    return pl.pallas_call(
-        prep_kernel,
+def middle_rows(probe, tile, left, right):
+    whole = pl.BlockSpec(memory_space=pltpu.VMEM)
+    return pl.pallas_call(
+        middle_kernel,
         out_shape=(
             jax.ShapeDtypeStruct((2, 2, 1, 2, HALF, HALF), f32),
-            jax.ShapeDtypeStruct((2, 2, BLOCKS, 2, EXT // 2, HALF), f32),
+            jax.ShapeDtypeStruct((2, 2, BLOCKS, 2, TILE // 2, HALF), f32),
         ),
-        in_specs=[pl.BlockSpec(memory_space=pl.ANY)] * 6 + [pl.BlockSpec(memory_space=pltpu.VMEM)],
-        out_specs=[pl.BlockSpec(memory_space=pltpu.VMEM)] * 2,
-        scratch_shapes=[pltpu.VMEM((EXT, HALF), f32)] * 2
-        + [pltpu.VMEM(x.shape, f32) for x in (probe, *pieces)]
-        + [pltpu.SemaphoreType.DMA((6,))],
-        compiler_params=pltpu.CompilerParams(vmem_limit_bytes=40 << 20),
-        cost_estimate=pl.CostEstimate(flops=6 * EXT * EXT * PATCH * 2, bytes_accessed=16 * EXT * EXT, transcendentals=0),
-    )(probe, *pieces, jnp.asarray(shuffle()))
+        in_specs=[whole] * 5,
+        out_specs=[whole] * 2,
+        scratch_shapes=[pltpu.VMEM((TILE, HALF), f32)] * 2,
+        compiler_params=pltpu.CompilerParams(vmem_limit_bytes=30 << 20),
+        cost_estimate=pl.CostEstimate(flops=6 * TILE * EXT * PATCH * 2, bytes_accessed=16 * TILE * EXT, transcendentals=0),
+    )(probe, tile, left, right, jnp.asarray(shuffle()))
+
+
+def ends_kernel(up_ref, down_ref, perm_ref, out_ref, even_ref, odd_ref):
+    for side, ref in enumerate((up_ref, down_ref)):
+        for c in range(2):
+            for b in range(BLOCKS):
+                spread(ref[c, :, b * PATCH : (b + 1) * PATCH], perm_ref, out_ref.at[side], c, b, even_ref, odd_ref)
+
+
+def end_rows(up, down):
+    whole = pl.BlockSpec(memory_space=pltpu.VMEM)
+    return pl.pallas_call(
+        ends_kernel,
+        out_shape=jax.ShapeDtypeStruct((2, 2, 2, BLOCKS, 2, HALF // 2, HALF), f32),
+        in_specs=[whole] * 3,
+        out_specs=whole,
+        scratch_shapes=[pltpu.VMEM((HALF, HALF), f32)] * 2,
+        compiler_params=pltpu.CompilerParams(vmem_limit_bytes=30 << 20),
+        cost_estimate=pl.CostEstimate(flops=6 * PATCH * EXT * PATCH * 2, bytes_accessed=16 * PATCH * EXT, transcendentals=0),
+    )(up, down, jnp.asarray(shuffle()))
 
 
 def window(pos_ref, t):
@@ -164,8 +174,21 @@
     )
 
 
-def forward_kernel(pos_ref, count_ref, obj_ref, probe_ref, left_ref, right_ref, out_ref, *scratch):
+def forward_kernel(pos_ref, count_ref, middle_ref, ends_ref, probe_ref, left_ref, right_ref, out_ref, obj_ref, sem, *scratch):
     step = pl.program_id(0)
+
+    @pl.when(step == 0)
+    def _():
+        end = HALF // 2
+        spans = ((ends_ref.at[0], 0, end), (middle_ref, end, TILE // 2), (ends_ref.at[1], end + TILE // 2, end))
+        copies = [
+            pltpu.make_async_copy(source, obj_ref.at[:, :, :, :, pl.ds(first, size), :], sem.at[k])
+            for k, (source, first, size) in enumerate(spans)
+        ]
+        for copy in copies:
+            copy.start()
+        for copy in copies:
+            copy.wait()
 
     @pl.when(2 * step < count_ref[0])
     def _():
@@ -206,7 +229,7 @@
             out_ref[k, 1] = even - odd
 
 
-def forward(pos, count, obj, probe, lefts, rights):
+def forward(pos, count, middle, ends, probe, lefts, rights):
     whole = pl.BlockSpec(memory_space=pltpu.VMEM)
     return pl.pallas_call(
         forward_kernel,
@@ -214,13 +237,14 @@
         grid_spec=pltpu.PrefetchScalarGridSpec(
             num_scalar_prefetch=2,
             grid=(TASKS // 2,),
-            in_specs=[whole] * 4,
+            in_specs=[pl.BlockSpec(memory_space=pl.ANY)] * 2 + [whole] * 3,
             out_specs=pl.BlockSpec((2, 2, PATCH, PATCH), lambda t, pos, count: (t, 0, 0, 0)),
-            scratch_shapes=[pltpu.VMEM((2, PATCH, PATCH), bf16)] * 8,
+            scratch_shapes=[pltpu.VMEM((2, 2, BLOCKS, 2, EXT // 2, HALF), f32), pltpu.SemaphoreType.DMA((3,))]
+            + [pltpu.VMEM((2, PATCH, PATCH), bf16)] * 8,
         ),
         compiler_params=pltpu.CompilerParams(vmem_limit_bytes=40 << 20),
         cost_estimate=pl.CostEstimate(flops=TASKS * 24 * PATCH**3, bytes_accessed=TASKS * 8 * PATCH**2, transcendentals=0),
-    )(pos, count, obj, probe, lefts, rights)
+    )(pos, count, middle, ends, probe, lefts, rights)
 
 
 def inverse_kernel(last, pos_ref, order_ref, slot_ref, count_ref, far_0, far_1, frame_0, frame_1, probe_ref, left_ref, right_ref, *rest):
@@ -339,7 +363,7 @@
             out_specs=[whole] * 5 if last else whole,
             scratch_shapes=[pltpu.VMEM((2, PATCH, PATCH), bf16)] * 8 + (strips if last else []),
         ),
-        compiler_params=pltpu.CompilerParams(vmem_limit_bytes=40 << 20),
+        compiler_params=pltpu.CompilerParams(vmem_limit_bytes=(40 if last else 44) << 20),
         cost_estimate=pl.CostEstimate(flops=most * 24 * PATCH**3, bytes_accessed=most * 12 * PATCH**2, transcendentals=0),
     )(pos, order, slot, count, far, far, frames, frames, probe, lefts, rights, *more)
 
@@ -443,8 +467,10 @@
     order_0 = ordered(jnp.logical_and(valid, jnp.logical_not(second)), helper_cols, 16)
     order_1 = ordered(jnp.logical_and(valid, second), helper_cols, TASKS // 2)
     lefts, rights = tables()
-    pro, obj = prep(probe, pieces)
-    far = forward(offsets, count, obj, pro, lefts, rights)
+    tile, left, right, up, down = pieces
+    pro, middle = middle_rows(probe, tile, left, right)
+    ends = end_rows(up, down)
+    far = forward(offsets, count, middle, ends, pro, lefts, rights)
     part = inverse(False, 16, offsets, *order_0, far, arrived_0, pro, lefts, rights)
     return inverse(True, TASKS // 2, offsets, *order_1, far, arrived_1, pro, lefts, rights, part)
 

time: 242 us -> 234 us (0.967)
  waiting for transfers between devices: 85.2 us -> 80.6 us
  local copies, waits for them, and re-layouts: 8.58 us -> 4.77 us
    ppermute x4, waiting for transfers between devices: 16.4 us -> 12.5 us  [from_tile(): lax.ppermute(sent, 'gy', [(i + dy, i) for i in range(high) if 0 <= i + dy...]
    unnamed x33 -> x31, local copies, waits for them, and re-layouts: 7.11 us -> 3.27 us
  transfers between devices with their start and end apart: 11 -> 11, of which waited for: 8 -> 8; matrix products, arithmetic and copies ran while one was open for 2% -> 1% of each run, Pallas kernels for 14% -> 15%
where the time goes in v4:
time: 234 us; the launch traced here: 232 us
  waiting for transfers between devices  80.6 us (34%)
  Pallas kernels  54.8 us (23%)
  blocking collectives  53.2 us (23%)
  starting transfers between devices  36.1 us (15%)
  local copies, waits for them, and re-layouts  4.77 us (2%)
    ppermute x6, waiting for transfers between devices, from_tile(): lax.ppermute(sent, 'gx', [(i + dx, i) for i in range(wide) if 0 <= i + dx...  68 us
    all_to_all x1, blocking collectives, per_device(): lax.all_to_all(pick(kept, 0), 'gx', split_axis=0, concat_axis=0, tiled=True)  53.2 us
    pallas_call x2, Pallas kernels, inverse(): pl.pallas_call(functools.partial(inverse_kernel, last), out_shape=[jax.Sh...  24.3 us
    pallas_call x1, Pallas kernels, forward(): pl.pallas_call(forward_kernel, out_shape=jax.ShapeDtypeStruct((TASKS, 2,...  16.2 us
    ppermute x6, starting transfers between devices, from_tile(): lax.ppermute(sent, 'gx', [(i + dx, i) for i in range(wide) if 0 <= i + dx...  16 us
    ppermute x4, waiting for transfers between devices, from_tile(): lax.ppermute(sent, 'gy', [(i + dy, i) for i in range(high) if 0 <= i + dy...  12.5 us
    ppermute x4, starting transfers between devices, from_tile(): lax.ppermute(sent, 'gy', [(i + dy, i) for i in range(high) if 0 <= i + dy...  12.3 us
    all_to_all x1, starting transfers between devices, per_device(): lax.all_to_all(pick(again, 1), 'gx', split_axis=0, concat_axis=0, tiled=T...  7.81 us
  transfers between devices with their start and end apart: 11, of which 8 were waited for; matrix products, arithmetic and copies ran while one was open for 1% of the time, Pallas kernels for 15%

profile of v4, /device:TPU:91, one launch (start us, length us, event | category | flops | bytes accessed | tf_op | source)
XLA Modules:
  0.0 231.8 jit_solution(11812955106202371484)
XLA Ops:
  0.0 3.3 %shard_map.113 = f32[16,256,256]{2,1,0:T(8,128)} custom-call(f32[16,2,256,256]{3,2,1,0:T(8,128)} %bitcast.10), custom_call_target="tpu_custom_call" | custom-call | bytes 8388608 | tf_op jit(solution)/shard_map/pallas_call | solution.py:413
  3.3 53.2 %all_to_all.10.frame_0.frame_1 = f32[16,256,256]{2,1,0:T(8,128)} all-to-all(f32[16,256,256]{2,1,0:T(8,128)} %shard_map.113), channel_id=1, replica_groups=mesh['gx'=16,'gy'=8] {'gx'}, dimensions={0} | all-to-all | bytes 8388608 | tf_op jit(solution)/shard_map/all_to_all | solution.py:482
  56.5 3.3 %shard_map.114 = f32[16,256,256]{2,1,0:T(8,128)} custom-call(f32[16,2,256,256]{3,2,1,0:T(8,128)} %bitcast.11), custom_call_target="tpu_custom_call" | custom-call | bytes 8388608 | tf_op jit(solution)/shard_map/pallas_call | solution.py:413
  59.8 7.8 %all-to-all-start.1 = ((f32[16,256,256]{2,1,0:T(8,128)}), f32[16,256,256]{2,1,0:T(8,128)}, u32[]{:S(2)}, u32[]{:S(2)}) async-start(f32[16,256,256]{2,1,0:T(8,128)} %shard_map.114), calls=%async_computation.1 | async-start | bytes 8388608 | tf_op jit(solution)/shard_map/all_to_all | solution.py:484
  67.7 2.2 shard_map.109
  69.9 2.9 %collective-permute-start = (f32[2,512,128]{2,1,0:T(8,128)}, f32[2,512,128]{2,1,0:T(8,128)S(1)}, u32[]{:S(2)}, u32[]{:S(2)}) collective-permute-start(f32[2,512,128]{2,1,0:T(8,128)} %get-tuple-element.15), channel_id=1, source_target_pairs={{0,8},{8,16},{16,24},{24,32},{32,40},{40,48},{48,56},{56,64},{64,7... | collective-permute-start | bytes 1572872 | tf_op jit(solution)/shard_map/ppermute | solution.py:427
  72.9 2.5 %collective-permute-start.1 = (f32[2,512,128]{2,1,0:T(8,128)}, f32[2,512,128]{2,1,0:T(8,128)S(1)}, u32[]{:S(2)}, u32[]{:S(2)}) collective-permute-start(f32[2,512,128]{2,1,0:T(8,128)} %get-tuple-element.16), channel_id=1, source_target_pairs={{8,0},{16,8},{24,16},{32,24},{40,32},{48,40},{56,48},{64,56},{72,6... | collective-permute-start | bytes 1572872 | tf_op jit(solution)/shard_map/ppermute | solution.py:427
  77.6 60.0 %collective-permute-done.left_ref = f32[2,512,128]{2,1,0:T(8,128)S(1)} collective-permute-done((f32[2,512,128]{2,1,0:T(8,128)}, f32[2,512,128]{2,1,0:T(8,128)S(1)}, u32[]{:S(2)}, u32[]{:S(2)}) %collective-permute-start) | collective-permute-done | bytes 524320 | tf_op jit(solution)/shard_map/ppermute | solution.py:427
  137.7 5.9 %collective-permute-start.2 = (f32[2,128,768]{2,1,0:T(8,128)S(1)}, f32[2,128,768]{2,1,0:T(8,128)S(1)}, u32[]{:S(2)}, u32[]{:S(2)}) collective-permute-start(f32[2,128,768]{2,1,0:T(8,128)S(1)} %pad_maximum_fusion), channel_id=1, source_target_pairs={{0,1},{1,2},{2,3},{3,4},{4,5},{5,6},{6,7},{8,9},{9,10},{10,11},{11... | collective-permute-start | bytes 2359304 | tf_op jit(solution)/shard_map/ppermute | solution.py:428
  143.7 2.1 collective-permute-start.3
  149.1 2.1 shard_map.110
  152.5 4.6 %collective-permute-done.3.down_ref = f32[2,128,768]{2,1,0:T(8,128)S(1)} collective-permute-done((f32[2,128,768]{2,1,0:T(8,128)S(1)}, f32[2,128,768]{2,1,0:T(8,128)S(1)}, u32[]{:S(2)}, u32[]{:S(2)}) %collective-permute-start.3) | collective-permute-done | bytes 786464 | tf_op jit(solution)/shard_map/ppermute | solution.py:428
  158.1 16.2 %shard_map.112.far_0.far_1 = f32[24,2,256,256]{3,2,1,0:T(8,128)} custom-call(s32[48]{0:T(128)S(1)} %reshape_squeeze.3.pos_ref, s32[1]{0:T(128)} %bitcast.9.count_ref, f32[2,2,3,2,256,128]{5,4,3,2,1,0:T(8,128)S(1)} %get-tuple-element.17.middle_ref, f32[2,2,2,3,2,64,128]{6,5,4,3,2,1,0:T(8,128)S(1)} %shard_map.111.ends_ref, ...), custom_call_target="tpu_custom_call" | custom-call | flops 9663676416 | bytes 12582912 | tf_op jit(solution)/shard_map/pallas_call | solution.py:234
  174.4 13.9 %shard_map.115.rest_1_ = f32[2,2,3,2,384,128]{5,4,3,2,1,0:T(8,128)} custom-call(s32[48]{0:T(128)S(1)} %reshape_squeeze.3.pos_ref, s32[16]{0:T(128)S(1)} %get-tuple-element.26.order_ref, s32[16]{0:T(128)S(1)} %get-tuple-element.25.slot_ref, s32[1]{0:T(128)} %bitcast.5.count_ref, f32[24,2,256,256]{3,2,1,0:T(8,128)} %shard_map.112.far_0.far_1, ...), custom_call_target="tpu_custom_call" | custom-call | flops 6442450944 | bytes 12582912 | tf_op jit(solution)/shard_map/pallas_call | solution.py:356
  189.3 10.4 %shard_map.116 = (f32[2,512,512]{2,1,0:T(8,128)S(1)}, f32[2,512,128]{2,1,0:T(8,128)S(1)}, f32[2,512,128]{2,1,0:T(8,128)S(1)}, f32[2,128,768]{2,1,0:T(8,128)S(1)}, f32[2,128,768]{2,1,0:T(8,128)S(1)}) custom-call(s32[48]{0:T(128)S(1)} %reshape_squeeze.3.pos_ref, s32[12]{0:T(128)S(1)} %get-tuple-element.28.order_ref, s32[12]{0:T(128)S(1)} %get-tuple-element.27.slot_ref, ...), custom_call_target="tpu_custom_call" | custom-call | flops 4831838208 | bytes 9437184 | tf_op jit(solution)/shard_map/pallas_call | solution.py:356
  199.7 1.9 collective-permute-start.6
  201.6 2.4 %collective-permute-start.7 = (f32[2,128,768]{2,1,0:T(8,128)S(1)}, f32[2,128,768]{2,1,0:T(8,128)S(1)}, u32[]{:S(2)}, u32[]{:S(2)}) collective-permute-start(f32[2,128,768]{2,1,0:T(8,128)S(1)} %get-tuple-element.24), channel_id=1, source_target_pairs={{1,0},{2,1},{3,2},{4,3},{5,4},{6,5},{7,6},{9,8},{10,9},{11,10},{12... | collective-permute-start | bytes 2359304 | tf_op jit(solution)/shard_map/ppermute | solution.py:428
  204.0 1.9 collective-permute-start.4
  206.0 3.4 %collective-permute-start.5 = (f32[2,512,128]{2,1,0:T(8,128)S(1)}, f32[2,512,128]{2,1,0:T(8,128)S(1)}, u32[]{:S(2)}, u32[]{:S(2)}) collective-permute-start(f32[2,512,128]{2,1,0:T(8,128)S(1)} %get-tuple-element.22), channel_id=1, source_target_pairs={{8,0},{16,8},{24,16},{32,24},{40,32},{48,40},{56,48},{64,56},{72,6... | collective-permute-start | bytes 1572872 | tf_op jit(solution)/shard_map/ppermute | solution.py:427
  210.6 5.5 %collective-permute-done.7.down_ref = f32[2,128,768]{2,1,0:T(8,128)S(1)} collective-permute-done((f32[2,128,768]{2,1,0:T(8,128)S(1)}, f32[2,128,768]{2,1,0:T(8,128)S(1)}, u32[]{:S(2)}, u32[]{:S(2)}) %collective-permute-start.7) | collective-permute-done | bytes 786464 | tf_op jit(solution)/shard_map/ppermute | solution.py:428
  218.1 3.4 %collective-permute-start.9 = (f32[2,256,128]{2,1,0:T(8,128)S(1)}, f32[2,256,128]{2,1,0:T(8,128)S(1)}, u32[]{:S(2)}, u32[]{:S(2)}) collective-permute-start(f32[2,256,128]{2,1,0:T(8,128)S(1)} %pad_maximum_fusion.3), channel_id=1, source_target_pairs={{8,0},{16,8},{24,16},{32,24},{40,32},{48,40},{56,48},{64,56},{72,6... | collective-permute-start | bytes 786440 | tf_op jit(solution)/shard_map/ppermute | solution.py:427
  222.0 3.7 %collective-permute-done.8.left_ends = f32[2,256,128]{2,1,0:T(8,128)S(1)} collective-permute-done((f32[2,256,128]{2,1,0:T(8,128)S(1)}, f32[2,256,128]{2,1,0:T(8,128)S(1)}, u32[]{:S(2)}, u32[]{:S(2)}) %collective-permute-start.8) | collective-permute-done | bytes 262176 | tf_op jit(solution)/shard_map/ppermute | solution.py:427
  225.7 3.8 %collective-permute-done.9.right_ends = f32[2,256,128]{2,1,0:T(8,128)S(1)} collective-permute-done((f32[2,256,128]{2,1,0:T(8,128)S(1)}, f32[2,256,128]{2,1,0:T(8,128)S(1)}, u32[]{:S(2)}, u32[]{:S(2)}) %collective-permute-start.9) | collective-permute-done | bytes 262176 | tf_op jit(solution)/shard_map/ppermute | solution.py:427
  229.5 2.3 shard_map.117
  (54 shorter events, 12.0 us)
Async XLA Ops:
  59.8 16.2 %copy-start.14 = (s32[1,1,24,2]{2,3,1,0:T(2,128)S(1)}, s32[1,1,24,2]{2,3,1,0:T(2,128)}, u32[]{:S(2)}) copy-start(s32[1,1,24,2]{2,3,1,0:T(2,128)} %param.14) | copy-start | bytes 580
  59.8 128.4 %all-to-all-start.1 = ((f32[16,256,256]{2,1,0:T(8,128)}), f32[16,256,256]{2,1,0:T(8,128)}, u32[]{:S(2)}, u32[]{:S(2)}) async-start(f32[16,256,256]{2,1,0:T(8,128)} %shard_map.114), calls=%async_computation.1 | async-start | bytes 8388608 | tf_op jit(solution)/shard_map/all_to_all | solution.py:484
  67.7 78.1 %copy-start.13 = (s32[1,1,24,1]{2,3,1,0:T(1,128)S(1)}, s32[1,1,24,1]{2,3,1,0:T(1,128)}, u32[]{:S(2)}) copy-start(s32[1,1,24,1]{2,3,1,0:T(1,128)} %param.15) | copy-start | bytes 292
  67.7 79.4 %copy-start.7 = (bf16[256,256]{1,0:T(8,128)(2,1)S(1)}, bf16[256,256]{1,0:T(8,128)(2,1)}, u32[]{:S(2)}) copy-start(bf16[256,256]{1,0:T(8,128)(2,1)} %constant.14.clone.perm_ref) | copy-start | bytes 393220
  69.9 77.1 %copy-start.1 = (f32[2,512,512]{2,1,0:T(8,128)S(1)}, f32[2,512,512]{2,1,0:T(8,128)}, u32[]{:S(2)}) copy-start(f32[2,512,512]{2,1,0:T(8,128)} %object_ref.3) | copy-start | bytes 6291460
  69.9 67.6 %collective-permute-start = (f32[2,512,128]{2,1,0:T(8,128)}, f32[2,512,128]{2,1,0:T(8,128)S(1)}, u32[]{:S(2)}, u32[]{:S(2)}) collective-permute-start(f32[2,512,128]{2,1,0:T(8,128)} %get-tuple-element.15), channel_id=1, source_target_pairs={{0,8},{8,16},{16,24},{24,32},{32,40},{40,48},{48,56},{56,64},{64,7... | collective-permute-start | bytes 1572872 | tf_op jit(solution)/shard_map/ppermute | solution.py:427
  72.9 64.7 %collective-permute-start.1 = (f32[2,512,128]{2,1,0:T(8,128)}, f32[2,512,128]{2,1,0:T(8,128)S(1)}, u32[]{:S(2)}, u32[]{:S(2)}) collective-permute-start(f32[2,512,128]{2,1,0:T(8,128)} %get-tuple-element.16), channel_id=1, source_target_pairs={{8,0},{16,8},{24,16},{32,24},{40,32},{48,40},{56,48},{64,56},{72,6... | collective-permute-start | bytes 1572872 | tf_op jit(solution)/shard_map/ppermute | solution.py:427
  76.2 70.8 %copy-start.12 = (f32[2,256,256]{2,1,0:T(8,128)S(1)}, f32[2,256,256]{2,1,0:T(8,128)}, u32[]{:S(2)}) copy-start(f32[2,256,256]{2,1,0:T(8,128)} %probe_ref.1) | copy-start | bytes 1572868
  137.6 6.0 %copy-start.8 = (f32[2,512,128]{2,1,0:T(8,128)}, f32[2,512,128]{2,1,0:T(8,128)S(1)}, u32[]{:S(2)}) copy-start(f32[2,512,128]{2,1,0:T(8,128)S(1)} %collective-permute-done.left_ref) | copy-start | bytes 1572868
  137.6 6.0 %copy-start.10 = (f32[2,512,128]{2,1,0:T(8,128)}, f32[2,512,128]{2,1,0:T(8,128)S(1)}, u32[]{:S(2)}) copy-start(f32[2,512,128]{2,1,0:T(8,128)S(1)} %collective-permute-done.1.right_ref) | copy-start | bytes 1572868
  137.7 14.8 %collective-permute-start.2 = (f32[2,128,768]{2,1,0:T(8,128)S(1)}, f32[2,128,768]{2,1,0:T(8,128)S(1)}, u32[]{:S(2)}, u32[]{:S(2)}) collective-permute-start(f32[2,128,768]{2,1,0:T(8,128)S(1)} %pad_maximum_fusion), channel_id=1, source_target_pairs={{0,1},{1,2},{2,3},{3,4},{4,5},{5,6},{6,7},{8,9},{9,10},{10,11},{11... | collective-permute-start | bytes 2359304 | tf_op jit(solution)/shard_map/ppermute | solution.py:428
  143.7 14.5 %copy-start.2 = (bf16[2,2,256,256]{3,2,1,0:T(8,128)(2,1)S(1)}, bf16[2,2,256,256]{3,2,1,0:T(8,128)(2,1)}, u32[]{:S(2)}) copy-start(bf16[2,2,256,256]{3,2,1,0:T(8,128)(2,1)} %constant.13.clone.right_ref) | copy-start | bytes 1572868
  143.7 14.5 %copy-start.3 = (bf16[2,2,256,256]{3,2,1,0:T(8,128)(2,1)S(1)}, bf16[2,2,256,256]{3,2,1,0:T(8,128)(2,1)}, u32[]{:S(2)}) copy-start(bf16[2,2,256,256]{3,2,1,0:T(8,128)(2,1)} %constant.12.clone.left_ref) | copy-start | bytes 1572868
  143.7 13.4 %collective-permute-start.3 = (f32[2,128,768]{2,1,0:T(8,128)S(1)}, f32[2,128,768]{2,1,0:T(8,128)S(1)}, u32[]{:S(2)}, u32[]{:S(2)}) collective-permute-start(f32[2,128,768]{2,1,0:T(8,128)S(1)} %pad_maximum_fusion.1), channel_id=1, source_target_pairs={{1,0},{2,1},{3,2},{4,3},{5,4},{6,5},{7,6},{9,8},{10,9},{11,10},{12... | collective-permute-start | bytes 2359304 | tf_op jit(solution)/shard_map/ppermute | solution.py:428
  151.3 23.1 %copy-start.4 = (f32[2,2,1,2,128,128]{5,4,3,2,1,0:T(8,128)}, f32[2,2,1,2,128,128]{5,4,3,2,1,0:T(8,128)S(1)}, u32[]{:S(2)}) copy-start(f32[2,2,1,2,128,128]{5,4,3,2,1,0:T(8,128)S(1)} %get-tuple-element.18.probe_ref) | copy-start | bytes 1572868
  158.1 16.2 %copy-start = (f32[16,256,256]{2,1,0:T(8,128)S(1)}, f32[16,256,256]{2,1,0:T(8,128)}, u32[]{:S(2)}) copy-start(f32[16,256,256]{2,1,0:T(8,128)} %all_to_all.10.frame_0.frame_1) | copy-start | bytes 12582916
  174.4 13.9 %copy-start.6 = (bf16[256,256]{1,0:T(8,128)(2,1)S(1)}, bf16[256,256]{1,0:T(8,128)(2,1)}, u32[]{:S(2)}) copy-start(bf16[256,256]{1,0:T(8,128)(2,1)} %constant.15.clone.rest_0_) | copy-start | bytes 393220
  188.3 1.0 copy-start.5
  199.7 10.8 %collective-permute-start.6 = (f32[2,128,768]{2,1,0:T(8,128)S(1)}, f32[2,128,768]{2,1,0:T(8,128)S(1)}, u32[]{:S(2)}, u32[]{:S(2)}) collective-permute-start(f32[2,128,768]{2,1,0:T(8,128)S(1)} %get-tuple-element.23), channel_id=1, source_target_pairs={{0,1},{1,2},{2,3},{3,4},{4,5},{5,6},{6,7},{8,9},{9,10},{10,11},{11... | collective-permute-start | bytes 2359304 | tf_op jit(solution)/shard_map/ppermute | solution.py:428
  201.6 14.4 %collective-permute-start.7 = (f32[2,128,768]{2,1,0:T(8,128)S(1)}, f32[2,128,768]{2,1,0:T(8,128)S(1)}, u32[]{:S(2)}, u32[]{:S(2)}) collective-permute-start(f32[2,128,768]{2,1,0:T(8,128)S(1)} %get-tuple-element.24), channel_id=1, source_target_pairs={{1,0},{2,1},{3,2},{4,3},{5,4},{6,5},{7,6},{9,8},{10,9},{11,10},{12... | collective-permute-start | bytes 2359304 | tf_op jit(solution)/shard_map/ppermute | solution.py:428
  204.0 17.4 %collective-permute-start.4 = (f32[2,512,128]{2,1,0:T(8,128)S(1)}, f32[2,512,128]{2,1,0:T(8,128)S(1)}, u32[]{:S(2)}, u32[]{:S(2)}) collective-permute-start(f32[2,512,128]{2,1,0:T(8,128)S(1)} %get-tuple-element.21), channel_id=1, source_target_pairs={{0,8},{8,16},{16,24},{24,32},{32,40},{40,48},{48,56},{56,64},{64,7... | collective-permute-start | bytes 1572872 | tf_op jit(solution)/shard_map/ppermute | solution.py:427
  206.0 16.0 %collective-permute-start.5 = (f32[2,512,128]{2,1,0:T(8,128)S(1)}, f32[2,512,128]{2,1,0:T(8,128)S(1)}, u32[]{:S(2)}, u32[]{:S(2)}) collective-permute-start(f32[2,512,128]{2,1,0:T(8,128)S(1)} %get-tuple-element.22), channel_id=1, source_target_pairs={{8,0},{16,8},{24,16},{32,24},{40,32},{48,40},{56,48},{64,56},{72,6... | collective-permute-start | bytes 1572872 | tf_op jit(solution)/shard_map/ppermute | solution.py:427
  216.1 9.6 %collective-permute-start.8 = (f32[2,256,128]{2,1,0:T(8,128)S(1)}, f32[2,256,128]{2,1,0:T(8,128)S(1)}, u32[]{:S(2)}, u32[]{:S(2)}) collective-permute-start(f32[2,256,128]{2,1,0:T(8,128)S(1)} %pad_maximum_fusion.2), channel_id=1, source_target_pairs={{0,8},{8,16},{16,24},{24,32},{32,40},{40,48},{48,56},{56,64},{64,7... | collective-permute-start | bytes 786440 | tf_op jit(solution)/shard_map/ppermute | solution.py:427
  218.1 11.4 %collective-permute-start.9 = (f32[2,256,128]{2,1,0:T(8,128)S(1)}, f32[2,256,128]{2,1,0:T(8,128)S(1)}, u32[]{:S(2)}, u32[]{:S(2)}) collective-permute-start(f32[2,256,128]{2,1,0:T(8,128)S(1)} %pad_maximum_fusion.3), channel_id=1, source_target_pairs={{8,0},{16,8},{24,16},{32,24},{40,32},{48,40},{56,48},{64,56},{72,6... | collective-permute-start | bytes 786440 | tf_op jit(solution)/shard_map/ppermute | solution.py:427
  (2 other events, 2.1 us)

commit v5 on v4

--- a/solution.py
+++ b/solution.py
@@ -255,14 +255,16 @@
         acc_ref, even_ref, odd_ref, earlier_ref, sem = rest[15:]
         load = pltpu.make_async_copy(before_ref, earlier_ref, sem)
     else:
-        acc_ref = rest[0]
-        scratch = rest[1:]
+        acc_ref, probe_out = rest[:2]
+        scratch = rest[2:]
     i = pl.program_id(0)
 
     @pl.when(i == 0)
     def _():
         if last:
             load.start()
+        else:
+            probe_out[...] = probe_ref[...]
         acc_ref[...] = jnp.zeros_like(acc_ref)
 
     @pl.when(2 * i < count_ref[0])
@@ -355,12 +357,14 @@
 
     return pl.pallas_call(
         functools.partial(inverse_kernel, last),
-        out_shape=[jax.ShapeDtypeStruct((2,) + size, f32) for size in sizes] if last else jax.ShapeDtypeStruct(parts, f32),
+        out_shape=[jax.ShapeDtypeStruct((2,) + size, f32) for size in sizes]
+        if last
+        else [jax.ShapeDtypeStruct(parts, f32), jax.ShapeDtypeStruct(probe.shape, f32)],
         grid_spec=pltpu.PrefetchScalarGridSpec(
             num_scalar_prefetch=4,
             grid=(most // 2,),
             in_specs=[far_spec(0), far_spec(1), frame_spec(0), frame_spec(1)] + [whole] * 3 + more_specs,
-            out_specs=[whole] * 5 if last else whole,
+            out_specs=[whole] * (5 if last else 2),
             scratch_shapes=[pltpu.VMEM((2, PATCH, PATCH), bf16)] * 8 + (strips if last else []),
         ),
         compiler_params=pltpu.CompilerParams(vmem_limit_bytes=(40 if last else 44) << 20),
@@ -471,7 +475,7 @@
     pro, middle = middle_rows(probe, tile, left, right)
     ends = end_rows(up, down)
     far = forward(offsets, count, middle, ends, pro, lefts, rights)
-    part = inverse(False, 16, offsets, *order_0, far, arrived_0, pro, lefts, rights)
+    part, pro = inverse(False, 16, offsets, *order_0, far, arrived_0, pro, lefts, rights)
     return inverse(True, TASKS // 2, offsets, *order_1, far, arrived_1, pro, lefts, rights, part)
 
 

time: 234 us -> 236 us (level)
  transfers between devices with their start and end apart: 11 -> 11, of which waited for: 8 -> 7; matrix products, arithmetic and copies ran while one was open for 1% -> 1% of each run, Pallas kernels for 15% -> 15%
where the time goes in v5:
time: 236 us; the launch traced here: 232 us
  waiting for transfers between devices  78.3 us (33%)
  Pallas kernels  54.6 us (23%)
  blocking collectives  53.2 us (23%)
  starting transfers between devices  38.2 us (16%)
  local copies, waits for them, and re-layouts  5.5 us (2%)
    ppermute x6, waiting for transfers between devices, from_tile(): lax.ppermute(sent, 'gx', [(i + dx, i) for i in range(wide) if 0 <= i + dx...  65.8 us
    all_to_all x1, blocking collectives, per_device(): lax.all_to_all(pick(kept, 0), 'gx', split_axis=0, concat_axis=0, tiled=True)  53.2 us
    pallas_call x2, Pallas kernels, inverse(): pl.pallas_call(functools.partial(inverse_kernel, last), out_shape=[jax.Sh...  24.2 us
    ppermute x6, starting transfers between devices, from_tile(): lax.ppermute(sent, 'gx', [(i + dx, i) for i in range(wide) if 0 <= i + dx...  18.1 us
    pallas_call x1, Pallas kernels, forward(): pl.pallas_call(forward_kernel, out_shape=jax.ShapeDtypeStruct((TASKS, 2,...  16.1 us
    ppermute x4, waiting for transfers between devices, from_tile(): lax.ppermute(sent, 'gy', [(i + dy, i) for i in range(high) if 0 <= i + dy...  12.6 us
    ppermute x4, starting transfers between devices, from_tile(): lax.ppermute(sent, 'gy', [(i + dy, i) for i in range(high) if 0 <= i + dy...  12.3 us
    all_to_all x1, starting transfers between devices, per_device(): lax.all_to_all(pick(again, 1), 'gx', split_axis=0, concat_axis=0, tiled=T...  7.83 us
  transfers between devices with their start and end apart: 11, of which 7 were waited for; matrix products, arithmetic and copies ran while one was open for 1% of the time, Pallas kernels for 15%

profile of v5, /device:TPU:91, one launch (start us, length us, event | category | flops | bytes accessed | tf_op | source)
XLA Modules:
  0.0 232.2 jit_solution(13690671723185566929)
XLA Ops:
  0.0 3.3 %shard_map.113 = f32[16,256,256]{2,1,0:T(8,128)} custom-call(f32[16,2,256,256]{3,2,1,0:T(8,128)} %bitcast.10), custom_call_target="tpu_custom_call" | custom-call | bytes 8388608 | tf_op jit(solution)/shard_map/pallas_call | solution.py:417
  3.3 53.2 %all_to_all.10.frame_0.frame_1 = f32[16,256,256]{2,1,0:T(8,128)} all-to-all(f32[16,256,256]{2,1,0:T(8,128)} %shard_map.113), channel_id=1, replica_groups=mesh['gx'=16,'gy'=8] {'gx'}, dimensions={0} | all-to-all | bytes 8388608 | tf_op jit(solution)/shard_map/all_to_all | solution.py:486
  56.5 3.3 %shard_map.114 = f32[16,256,256]{2,1,0:T(8,128)} custom-call(f32[16,2,256,256]{3,2,1,0:T(8,128)} %bitcast.11), custom_call_target="tpu_custom_call" | custom-call | bytes 8388608 | tf_op jit(solution)/shard_map/pallas_call | solution.py:417
  59.8 7.8 %all-to-all-start.1 = ((f32[16,256,256]{2,1,0:T(8,128)}), f32[16,256,256]{2,1,0:T(8,128)}, u32[]{:S(2)}, u32[]{:S(2)}) async-start(f32[16,256,256]{2,1,0:T(8,128)} %shard_map.114), calls=%async_computation.1 | async-start | bytes 8388608 | tf_op jit(solution)/shard_map/all_to_all | solution.py:488
  67.7 2.2 shard_map.109
  69.9 2.9 %collective-permute-start = (f32[2,512,128]{2,1,0:T(8,128)}, f32[2,512,128]{2,1,0:T(8,128)S(1)}, u32[]{:S(2)}, u32[]{:S(2)}) collective-permute-start(f32[2,512,128]{2,1,0:T(8,128)} %get-tuple-element.17), channel_id=1, source_target_pairs={{0,8},{8,16},{16,24},{24,32},{32,40},{40,48},{48,56},{56,64},{64,7... | collective-permute-start | bytes 1572872 | tf_op jit(solution)/shard_map/ppermute | solution.py:431
  72.9 2.5 %collective-permute-start.1 = (f32[2,512,128]{2,1,0:T(8,128)}, f32[2,512,128]{2,1,0:T(8,128)S(1)}, u32[]{:S(2)}, u32[]{:S(2)}) collective-permute-start(f32[2,512,128]{2,1,0:T(8,128)} %get-tuple-element.18), channel_id=1, source_target_pairs={{8,0},{16,8},{24,16},{32,24},{40,32},{48,40},{56,48},{64,56},{72,6... | collective-permute-start | bytes 1572872 | tf_op jit(solution)/shard_map/ppermute | solution.py:431
  77.6 60.0 %collective-permute-done.left_ref = f32[2,512,128]{2,1,0:T(8,128)S(1)} collective-permute-done((f32[2,512,128]{2,1,0:T(8,128)}, f32[2,512,128]{2,1,0:T(8,128)S(1)}, u32[]{:S(2)}, u32[]{:S(2)}) %collective-permute-start) | collective-permute-done | bytes 524320 | tf_op jit(solution)/shard_map/ppermute | solution.py:431
  137.7 5.9 %collective-permute-start.2 = (f32[2,128,768]{2,1,0:T(8,128)S(1)}, f32[2,128,768]{2,1,0:T(8,128)S(1)}, u32[]{:S(2)}, u32[]{:S(2)}) collective-permute-start(f32[2,128,768]{2,1,0:T(8,128)S(1)} %pad_maximum_fusion), channel_id=1, source_target_pairs={{0,1},{1,2},{2,3},{3,4},{4,5},{5,6},{6,7},{8,9},{9,10},{10,11},{11... | collective-permute-start | bytes 2359304 | tf_op jit(solution)/shard_map/ppermute | solution.py:432
  143.7 2.1 collective-permute-start.3
  149.1 2.1 shard_map.110
  152.5 4.6 %collective-permute-done.3.down_ref = f32[2,128,768]{2,1,0:T(8,128)S(1)} collective-permute-done((f32[2,128,768]{2,1,0:T(8,128)S(1)}, f32[2,128,768]{2,1,0:T(8,128)S(1)}, u32[]{:S(2)}, u32[]{:S(2)}) %collective-permute-start.3) | collective-permute-done | bytes 786464 | tf_op jit(solution)/shard_map/ppermute | solution.py:432
  158.2 16.1 %shard_map.112.far_0.far_1 = f32[24,2,256,256]{3,2,1,0:T(8,128)} custom-call(s32[48]{0:T(128)S(1)} %reshape_squeeze.3.pos_ref, s32[1]{0:T(128)} %bitcast.9.count_ref, f32[2,2,3,2,256,128]{5,4,3,2,1,0:T(8,128)S(1)} %get-tuple-element.19.middle_ref, f32[2,2,2,3,2,64,128]{6,5,4,3,2,1,0:T(8,128)S(1)} %shard_map.111.ends_ref, ...), custom_call_target="tpu_custom_call" | custom-call | flops 9663676416 | bytes 12582912 | tf_op jit(solution)/shard_map/pallas_call | solution.py:234
  174.3 13.8 %shard_map.115 = (f32[2,2,3,2,384,128]{5,4,3,2,1,0:T(8,128)}, f32[2,2,1,2,128,128]{5,4,3,2,1,0:T(8,128)S(1)}) custom-call(s32[48]{0:T(128)S(1)} %reshape_squeeze.3.pos_ref, s32[16]{0:T(128)S(1)} %get-tuple-element.30.order_ref, s32[16]{0:T(128)S(1)} %get-tuple-element.29.slot_ref, s32[1]{0:T(128)} %bitcast.5.count_ref, ...), custom_call_target="tpu_custom_call" | custom-call | flops 6442450944 | bytes 12582912 | tf_op jit(solution)/shard_map/pallas_call | solution.py:358
  190.0 10.3 %shard_map.116 = (f32[2,512,512]{2,1,0:T(8,128)S(1)}, f32[2,512,128]{2,1,0:T(8,128)S(1)}, f32[2,512,128]{2,1,0:T(8,128)S(1)}, f32[2,128,768]{2,1,0:T(8,128)S(1)}, f32[2,128,768]{2,1,0:T(8,128)S(1)}) custom-call(s32[48]{0:T(128)S(1)} %reshape_squeeze.3.pos_ref, s32[12]{0:T(128)S(1)} %get-tuple-element.32.order_ref, s32[12]{0:T(128)S(1)} %get-tuple-element.31.slot_ref, ...), custom_call_target="tpu_custom_call" | custom-call | flops 4831838208 | bytes 9437184 | tf_op jit(solution)/shard_map/pallas_call | solution.py:358
  200.3 1.9 collective-permute-start.6
  202.3 2.4 %collective-permute-start.7 = (f32[2,128,768]{2,1,0:T(8,128)S(1)}, f32[2,128,768]{2,1,0:T(8,128)S(1)}, u32[]{:S(2)}, u32[]{:S(2)}) collective-permute-start(f32[2,128,768]{2,1,0:T(8,128)S(1)} %get-tuple-element.28), channel_id=1, source_target_pairs={{1,0},{2,1},{3,2},{4,3},{5,4},{6,5},{7,6},{9,8},{10,9},{11,10},{12... | collective-permute-start | bytes 2359304 | tf_op jit(solution)/shard_map/ppermute | solution.py:432
  204.7 1.9 collective-permute-start.4
  206.6 3.4 %collective-permute-start.5 = (f32[2,512,128]{2,1,0:T(8,128)S(1)}, f32[2,512,128]{2,1,0:T(8,128)S(1)}, u32[]{:S(2)}, u32[]{:S(2)}) collective-permute-start(f32[2,512,128]{2,1,0:T(8,128)S(1)} %get-tuple-element.26), channel_id=1, source_target_pairs={{8,0},{16,8},{24,16},{32,24},{40,32},{48,40},{56,48},{64,56},{72,6... | collective-permute-start | bytes 1572872 | tf_op jit(solution)/shard_map/ppermute | solution.py:431
  211.2 5.5 %collective-permute-done.7.down_ref = f32[2,128,768]{2,1,0:T(8,128)S(1)} collective-permute-done((f32[2,128,768]{2,1,0:T(8,128)S(1)}, f32[2,128,768]{2,1,0:T(8,128)S(1)}, u32[]{:S(2)}, u32[]{:S(2)}) %collective-permute-start.7) | collective-permute-done | bytes 786464 | tf_op jit(solution)/shard_map/ppermute | solution.py:432
  216.7 1.9 collective-permute-start.9
  218.7 5.5 %collective-permute-start.8 = (f32[2,256,128]{2,1,0:T(8,128)S(1)}, f32[2,256,128]{2,1,0:T(8,128)S(1)}, u32[]{:S(2)}, u32[]{:S(2)}) collective-permute-start(f32[2,256,128]{2,1,0:T(8,128)S(1)} %pad_maximum_fusion.2), channel_id=1, source_target_pairs={{0,8},{8,16},{16,24},{24,32},{32,40},{40,48},{48,56},{56,64},{64,7... | collective-permute-start | bytes 786440 | tf_op jit(solution)/shard_map/ppermute | solution.py:431
  224.2 4.9 %collective-permute-done.9.right_ends = f32[2,256,128]{2,1,0:T(8,128)S(1)} collective-permute-done((f32[2,256,128]{2,1,0:T(8,128)S(1)}, f32[2,256,128]{2,1,0:T(8,128)S(1)}, u32[]{:S(2)}, u32[]{:S(2)}) %collective-permute-start.9) | collective-permute-done | bytes 262176 | tf_op jit(solution)/shard_map/ppermute | solution.py:431
  229.9 2.3 shard_map.117
  (54 shorter events, 11.2 us)
Async XLA Ops:
  59.8 15.5 %copy-start.14 = (s32[1,1,24,2]{2,3,1,0:T(2,128)S(1)}, s32[1,1,24,2]{2,3,1,0:T(2,128)}, u32[]{:S(2)}) copy-start(s32[1,1,24,2]{2,3,1,0:T(2,128)} %param.14) | copy-start | bytes 580
  59.8 129.1 %all-to-all-start.1 = ((f32[16,256,256]{2,1,0:T(8,128)}), f32[16,256,256]{2,1,0:T(8,128)}, u32[]{:S(2)}, u32[]{:S(2)}) async-start(f32[16,256,256]{2,1,0:T(8,128)} %shard_map.114), calls=%async_computation.1 | async-start | bytes 8388608 | tf_op jit(solution)/shard_map/all_to_all | solution.py:488
  67.7 78.1 %copy-start.13 = (s32[1,1,24,1]{2,3,1,0:T(1,128)S(1)}, s32[1,1,24,1]{2,3,1,0:T(1,128)}, u32[]{:S(2)}) copy-start(s32[1,1,24,1]{2,3,1,0:T(1,128)} %param.15) | copy-start | bytes 292
  67.7 79.3 %copy-start.7 = (bf16[256,256]{1,0:T(8,128)(2,1)S(1)}, bf16[256,256]{1,0:T(8,128)(2,1)}, u32[]{:S(2)}) copy-start(bf16[256,256]{1,0:T(8,128)(2,1)} %constant.14.clone.perm_ref) | copy-start | bytes 393220
  69.9 77.1 %copy-start.1 = (f32[2,512,512]{2,1,0:T(8,128)S(1)}, f32[2,512,512]{2,1,0:T(8,128)}, u32[]{:S(2)}) copy-start(f32[2,512,512]{2,1,0:T(8,128)} %object_ref.3) | copy-start | bytes 6291460
  69.9 67.6 %collective-permute-start = (f32[2,512,128]{2,1,0:T(8,128)}, f32[2,512,128]{2,1,0:T(8,128)S(1)}, u32[]{:S(2)}, u32[]{:S(2)}) collective-permute-start(f32[2,512,128]{2,1,0:T(8,128)} %get-tuple-element.17), channel_id=1, source_target_pairs={{0,8},{8,16},{16,24},{24,32},{32,40},{40,48},{48,56},{56,64},{64,7... | collective-permute-start | bytes 1572872 | tf_op jit(solution)/shard_map/ppermute | solution.py:431
  72.9 64.7 %collective-permute-start.1 = (f32[2,512,128]{2,1,0:T(8,128)}, f32[2,512,128]{2,1,0:T(8,128)S(1)}, u32[]{:S(2)}, u32[]{:S(2)}) collective-permute-start(f32[2,512,128]{2,1,0:T(8,128)} %get-tuple-element.18), channel_id=1, source_target_pairs={{8,0},{16,8},{24,16},{32,24},{40,32},{48,40},{56,48},{64,56},{72,6... | collective-permute-start | bytes 1572872 | tf_op jit(solution)/shard_map/ppermute | solution.py:431
  75.6 71.4 %copy-start.12 = (f32[2,256,256]{2,1,0:T(8,128)S(1)}, f32[2,256,256]{2,1,0:T(8,128)}, u32[]{:S(2)}) copy-start(f32[2,256,256]{2,1,0:T(8,128)} %probe_ref.1) | copy-start | bytes 1572868
  137.6 6.0 %copy-start.8 = (f32[2,512,128]{2,1,0:T(8,128)}, f32[2,512,128]{2,1,0:T(8,128)S(1)}, u32[]{:S(2)}) copy-start(f32[2,512,128]{2,1,0:T(8,128)S(1)} %collective-permute-done.left_ref) | copy-start | bytes 1572868
  137.6 6.0 %copy-start.10 = (f32[2,512,128]{2,1,0:T(8,128)}, f32[2,512,128]{2,1,0:T(8,128)S(1)}, u32[]{:S(2)}) copy-start(f32[2,512,128]{2,1,0:T(8,128)S(1)} %collective-permute-done.1.right_ref) | copy-start | bytes 1572868
  137.7 14.8 %collective-permute-start.2 = (f32[2,128,768]{2,1,0:T(8,128)S(1)}, f32[2,128,768]{2,1,0:T(8,128)S(1)}, u32[]{:S(2)}, u32[]{:S(2)}) collective-permute-start(f32[2,128,768]{2,1,0:T(8,128)S(1)} %pad_maximum_fusion), channel_id=1, source_target_pairs={{0,1},{1,2},{2,3},{3,4},{4,5},{5,6},{6,7},{8,9},{9,10},{10,11},{11... | collective-permute-start | bytes 2359304 | tf_op jit(solution)/shard_map/ppermute | solution.py:432
  143.7 14.5 %copy-start.2 = (bf16[2,2,256,256]{3,2,1,0:T(8,128)(2,1)S(1)}, bf16[2,2,256,256]{3,2,1,0:T(8,128)(2,1)}, u32[]{:S(2)}) copy-start(bf16[2,2,256,256]{3,2,1,0:T(8,128)(2,1)} %constant.12.clone.left_ref) | copy-start | bytes 1572868
  143.7 14.5 %copy-start.3 = (bf16[2,2,256,256]{3,2,1,0:T(8,128)(2,1)S(1)}, bf16[2,2,256,256]{3,2,1,0:T(8,128)(2,1)}, u32[]{:S(2)}) copy-start(bf16[2,2,256,256]{3,2,1,0:T(8,128)(2,1)} %constant.13.clone.right_ref) | copy-start | bytes 1572868
  143.7 13.4 %collective-permute-start.3 = (f32[2,128,768]{2,1,0:T(8,128)S(1)}, f32[2,128,768]{2,1,0:T(8,128)S(1)}, u32[]{:S(2)}, u32[]{:S(2)}) collective-permute-start(f32[2,128,768]{2,1,0:T(8,128)S(1)} %pad_maximum_fusion.1), channel_id=1, source_target_pairs={{1,0},{2,1},{3,2},{4,3},{5,4},{6,5},{7,6},{9,8},{10,9},{11,10},{12... | collective-permute-start | bytes 2359304 | tf_op jit(solution)/shard_map/ppermute | solution.py:432
  147.0 1.0 copy-start.9
  158.1 16.2 %copy-start = (f32[16,256,256]{2,1,0:T(8,128)S(1)}, f32[16,256,256]{2,1,0:T(8,128)}, u32[]{:S(2)}) copy-start(f32[16,256,256]{2,1,0:T(8,128)} %all_to_all.10.frame_0.frame_1) | copy-start | bytes 12582916
  174.3 14.6 %copy-start.6 = (bf16[256,256]{1,0:T(8,128)(2,1)S(1)}, bf16[256,256]{1,0:T(8,128)(2,1)}, u32[]{:S(2)}) copy-start(bf16[256,256]{1,0:T(8,128)(2,1)} %constant.15.clone.rest_0_) | copy-start | bytes 393220
  189.0 1.0 copy-start.5
  200.3 10.8 %collective-permute-start.6 = (f32[2,128,768]{2,1,0:T(8,128)S(1)}, f32[2,128,768]{2,1,0:T(8,128)S(1)}, u32[]{:S(2)}, u32[]{:S(2)}) collective-permute-start(f32[2,128,768]{2,1,0:T(8,128)S(1)} %get-tuple-element.27), channel_id=1, source_target_pairs={{0,1},{1,2},{2,3},{3,4},{4,5},{5,6},{6,7},{8,9},{9,10},{10,11},{11... | collective-permute-start | bytes 2359304 | tf_op jit(solution)/shard_map/ppermute | solution.py:432
  202.3 14.4 %collective-permute-start.7 = (f32[2,128,768]{2,1,0:T(8,128)S(1)}, f32[2,128,768]{2,1,0:T(8,128)S(1)}, u32[]{:S(2)}, u32[]{:S(2)}) collective-permute-start(f32[2,128,768]{2,1,0:T(8,128)S(1)} %get-tuple-element.28), channel_id=1, source_target_pairs={{1,0},{2,1},{3,2},{4,3},{5,4},{6,5},{7,6},{9,8},{10,9},{11,10},{12... | collective-permute-start | bytes 2359304 | tf_op jit(solution)/shard_map/ppermute | solution.py:432
  204.7 19.5 %collective-permute-start.4 = (f32[2,512,128]{2,1,0:T(8,128)S(1)}, f32[2,512,128]{2,1,0:T(8,128)S(1)}, u32[]{:S(2)}, u32[]{:S(2)}) collective-permute-start(f32[2,512,128]{2,1,0:T(8,128)S(1)} %get-tuple-element.25), channel_id=1, source_target_pairs={{0,8},{8,16},{16,24},{24,32},{32,40},{40,48},{48,56},{56,64},{64,7... | collective-permute-start | bytes 1572872 | tf_op jit(solution)/shard_map/ppermute | solution.py:431
  206.6 17.5 %collective-permute-start.5 = (f32[2,512,128]{2,1,0:T(8,128)S(1)}, f32[2,512,128]{2,1,0:T(8,128)S(1)}, u32[]{:S(2)}, u32[]{:S(2)}) collective-permute-start(f32[2,512,128]{2,1,0:T(8,128)S(1)} %get-tuple-element.26), channel_id=1, source_target_pairs={{8,0},{16,8},{24,16},{32,24},{40,32},{48,40},{56,48},{64,56},{72,6... | collective-permute-start | bytes 1572872 | tf_op jit(solution)/shard_map/ppermute | solution.py:431
  216.7 12.3 %collective-permute-start.9 = (f32[2,256,128]{2,1,0:T(8,128)S(1)}, f32[2,256,128]{2,1,0:T(8,128)S(1)}, u32[]{:S(2)}, u32[]{:S(2)}) collective-permute-start(f32[2,256,128]{2,1,0:T(8,128)S(1)} %pad_maximum_fusion.3), channel_id=1, source_target_pairs={{8,0},{16,8},{24,16},{32,24},{40,32},{48,40},{56,48},{64,56},{72,6... | collective-permute-start | bytes 786440 | tf_op jit(solution)/shard_map/ppermute | solution.py:431
  218.7 11.3 %collective-permute-start.8 = (f32[2,256,128]{2,1,0:T(8,128)S(1)}, f32[2,256,128]{2,1,0:T(8,128)S(1)}, u32[]{:S(2)}, u32[]{:S(2)}) collective-permute-start(f32[2,256,128]{2,1,0:T(8,128)S(1)} %pad_maximum_fusion.2), channel_id=1, source_target_pairs={{0,8},{8,16},{16,24},{24,32},{32,40},{40,48},{48,56},{56,64},{64,7... | collective-permute-start | bytes 786440 | tf_op jit(solution)/shard_map/ppermute | solution.py:431
  (2 other events, 1.8 us)
